TPU v7x, 128 devices: a whole 4x4x4 slice. The times are simulated.
128 devices in a mesh: leaf: 128 (over z, y, x, core).
Axes of the slice: x: 4, y: 4, z: 4, core: 2. Of those that a mesh axis runs over, the one named last changes fastest.
Arguments:
- shots: float32 [131072, 2048], P('leaf'), may hold values from -6 to 6
- leaf_inverse: float32 [131072, 1024], P('leaf'), may hold values from -0.1875 to 0.1875
- leaf_basis: float32 [32768, 1024], P('leaf'), may hold values from -0.1875 to 0.1875
- leaf_back: float32 [131072, 256], P('leaf'), may hold values from -0.375 to 0.375
- level_one: float32 [32768, 1024], P('leaf'), may hold values from -0.25 to 0.25
- level_two: float32 [16384, 1024], P('leaf'), may hold values from -0.25 to 0.25
- level_three: float32 [8192, 1024], P('leaf'), may hold values from -0.25 to 0.25
- top_inverse: float32 [4096, 4096], P('leaf'), may hold values from -0.1 to 0.1, as said below
Outputs:
- solution: float32 [131072, 2048], P('leaf')
Inputs may be any that keep to these rules, and one draw needn't show every extreme that they name: top_inverse is symmetric.
All inputs are finite; a program needn't handle non-finite values.
Results may differ from a plain program's by a relative error of at most 0.0001.
Values sent between devices are 32-bit elements; how exact they have to be, the bound alone decides.
No kernel may reach another device: no remote copies, remote signals or barrier semaphores. Data moves between devices by JAX's collectives and lax.ppermute only.
A program may use at most 128 MiB of HBM per device.

v0:
```python
import jax
import jax.numpy as jnp
from jax import lax
from jax.sharding import PartitionSpec as P

LEVELS = 3


def partner_2(value, axis, bit):
    return lax.ppermute(value, axis, [(i, i ^ 1 << bit) for i in range(lax.axis_size(axis))])


def group_total(values, levels_up):
    for bit_number in range(levels_up):
        values = values + partner_2(values, "leaf", bit_number)
    return values


def group_rows(values, levels_up):
    position = lax.axis_index("leaf")
    for bit_number in range(levels_up):
        partner = partner_2(values, "leaf", bit_number)
        upper_half = position >> bit_number & 1 == 1
        values = jnp.where(
            upper_half, jnp.concatenate([partner, values], 0), jnp.concatenate([values, partner], 0)
        )
    return values


def collect_inverse(values, levels_up):
    position = lax.axis_index("leaf")
    for bit_number in range(levels_up):
        partner = partner_2(values, "leaf", bit_number)
        upper_half = position >> bit_number & 1 == 1
        values = jnp.where(
            upper_half, jnp.concatenate([partner, values], 0), jnp.concatenate([values, partner], 0)
        )
    return values


def collect_nodes(values, first_bit, bit_total):
    position = lax.axis_index("leaf")
    for bit_number in range(first_bit, bit_total):
        partner = partner_2(values, "leaf", bit_number)
        upper_half = position >> bit_number & 1 == 1
        values = jnp.where(
            upper_half, jnp.concatenate([partner, values], 0), jnp.concatenate([values, partner], 0)
        )
    return values


def collect_columns(values, levels_up):
    position = lax.axis_index("leaf")
    for bit_number in range(levels_up):
        partner = partner_2(values, "leaf", bit_number)
        upper_half = position >> bit_number & 1 == 1
        values = jnp.where(
            upper_half, jnp.concatenate([partner, values], 1), jnp.concatenate([values, partner], 1)
        )
    return values


def shards(
    shots, leaf_inverse, leaf_basis, leaf_back, level_one, level_two, level_three, top_inverse
):
    highest = lax.Precision.HIGHEST
    low_rank = leaf_basis.shape[0]
    position = lax.axis_index("leaf")
    solved = jnp.dot(leaf_inverse, shots, precision=highest)
    reduced = jnp.dot(leaf_basis, solved, precision=highest)
    stored = []
    for height, factors in enumerate((level_one, level_two, level_three)):
        partner = partner_2(reduced, "leaf", height)
        upper_half = position >> height & 1 == 1
        lower_child = jnp.where(upper_half, partner, reduced)
        upper_child = jnp.where(upper_half, reduced, partner)
        coupled = jnp.dot(factors[:, :low_rank], lower_child, precision=highest)
        coupled = coupled + jnp.dot(
            factors[:, low_rank : 2 * low_rank], upper_child, precision=highest
        )
        partial_term = lax.dot_general(
            factors[:, 2 * low_rank : 3 * low_rank],
            coupled,
            (((0,), (0,)), ((), ())),
            precision=highest,
        )
        reduced = group_total(partial_term, height + 1)
        stored.append((coupled, factors[:, 3 * low_rank :]))
    group_place = position % 2**LEVELS
    piece_width = reduced.shape[1] // 2**LEVELS
    shot_piece = lax.dynamic_slice_in_dim(reduced, group_place * piece_width, piece_width, 1)
    node_inverse = collect_inverse(top_inverse, LEVELS)
    all_pieces = collect_nodes(shot_piece, LEVELS, lax.axis_size("leaf").bit_length() - 1)
    solved_piece = jnp.dot(node_inverse, all_pieces, precision=highest)
    coefficient = collect_columns(solved_piece, LEVELS)
    for height in range(LEVELS - 1, -1, -1):
        coupled, back_block = stored[height]
        remainder = coupled - jnp.dot(back_block, coefficient, precision=highest)
        coefficient = group_rows(remainder, height)
    return solved - jnp.dot(leaf_back, coefficient, precision=highest)


def solution(mesh):
    return jax.shard_map(
        shards,
        mesh=mesh,
        in_specs=(
            P("leaf", None),
            P("leaf", None),
            P("leaf", None),
            P("leaf", None),
            P("leaf", None),
            P("leaf", None),
            P("leaf", None),
            P("leaf", None),
        ),
        out_specs=P("leaf", None),
        check_vma=False,
    )
```

profile of v0, /device:TPU:1, one launch (start us, length us, event | category | flops | bytes accessed | tf_op | source)
XLA Modules:
  0.0 531.6 jit_solution(13356029937029100561)
XLA Ops:
  0.0 29.9 %fusion.64 = f32[1024,2048]{1,0:T(8,128)S(1)} fusion(f32[1024,1024]{1,0:T(8,128)} %param.9, f32[1024,2048]{1,0:T(8,128)} %param.8), kind=kOutput, calls=%fused_computation.89 | convolution fusion | flops 25769803776 | bytes 20971520 | tf_op jit(solution)/shard_map/dot_general | solution.py:69
  29.9 13.4 %convolution_bitcast_fusion.3 = f32[256,2048]{0,1:T(8,128)S(1)} fusion(f32[1024,2048]{1,0:T(8,128)S(1)} %fusion.64, f32[256,1024]{1,0:T(8,128)S(1)} %copy-done.9), kind=kOutput, calls=%fused_computation.19 | convolution fusion | flops 6442450944 | bytes 11534336 | tf_op jit(solution)/shard_map/dot_general | solution.py:70
  44.9 3.9 collective-permute-done
  57.4 4.1 collective-permute-done.1
  63.6 45.9 %collective-permute-done.2 = f32[256,2048]{1,0:T(8,128)} collective-permute-done((f32[256,2048]{1,0:T(8,128)S(1)}, f32[256,2048]{1,0:T(8,128)}, u32[]{:S(2)}, u32[]{:S(2)}) %collective-permute-start.2) | collective-permute-done | bytes 2097184 | tf_op jit(solution)/shard_map/ppermute | solution.py:10
  109.5 5.1 fusion.31
  127.4 45.7 %collective-permute-done.4 = f32[256,2048]{0,1:T(8,128)S(1)} collective-permute-done((f32[256,2048]{0,1:T(8,128)S(1)}, f32[256,2048]{0,1:T(8,128)S(1)}, u32[]{:S(2)}, u32[]{:S(2)}) %collective-permute-start.4) | collective-permute-done | bytes 2097184 | tf_op jit(solution)/shard_map/ppermute | solution.py:10
  176.0 45.4 %collective-permute-done.5 = f32[256,2048]{0,1:T(8,128)} collective-permute-done((f32[256,2048]{0,1:T(8,128)S(1)}, f32[256,2048]{0,1:T(8,128)}, u32[]{:S(2)}, u32[]{:S(2)}) %collective-permute-start.5) | collective-permute-done | bytes 2097184 | tf_op jit(solution)/shard_map/ppermute | solution.py:10
  221.5 3.8 fusion.28
  236.6 45.7 %collective-permute-done.10 = f32[256,2048]{1,0:T(8,128)S(1)} collective-permute-done((f32[256,2048]{1,0:T(8,128)S(1)}, f32[256,2048]{1,0:T(8,128)S(1)}, u32[]{:S(2)}, u32[]{:S(2)}) %collective-permute-start.10) | collective-permute-done | bytes 2097184 | tf_op jit(solution)/shard_map/ppermute | solution.py:10
  286.5 43.6 %collective-permute-done.11 = f32[256,2048]{1,0:T(8,128)} collective-permute-done((f32[256,2048]{1,0:T(8,128)S(1)}, f32[256,2048]{1,0:T(8,128)}, u32[]{:S(2)}, u32[]{:S(2)}) %collective-permute-start.11) | collective-permute-done | bytes 2097184 | tf_op jit(solution)/shard_map/ppermute | solution.py:10
  332.5 4.4 collective-permute-done.12
  342.8 7.7 %collective-permute-done.13 = f32[512,256]{1,0:T(8,128)} collective-permute-done((f32[512,256]{1,0:T(8,128)S(1)}, f32[512,256]{1,0:T(8,128)}, u32[]{:S(2)}, u32[]{:S(2)}) %collective-permute-start.13) | collective-permute-done | bytes 524320 | tf_op jit(solution)/shard_map/ppermute | solution.py:10
  354.0 9.1 %collective-permute-done.7 = f32[64,4096]{1,0:T(8,128)} collective-permute-done((f32[64,4096]{1,0:T(8,128)S(1)}, f32[64,4096]{1,0:T(8,128)}, u32[]{:S(2)}, u32[]{:S(2)}) %collective-permute-start.7) | collective-permute-done | bytes 1048608 | tf_op jit(solution)/shard_map/ppermute | solution.py:10
  368.7 5.6 %collective-permute-done.14 = f32[1024,256]{1,0:T(8,128)} collective-permute-done((f32[1024,256]{1,0:T(8,128)S(1)}, f32[1024,256]{1,0:T(8,128)}, u32[]{:S(2)}, u32[]{:S(2)}) %collective-permute-start.14) | collective-permute-done | bytes 1048608 | tf_op jit(solution)/shard_map/ppermute | solution.py:10
  381.0 30.0 %collective-permute-done.8 = f32[128,4096]{1,0:T(8,128)} collective-permute-done((f32[128,4096]{1,0:T(8,128)}, f32[128,4096]{1,0:T(8,128)}, u32[]{:S(2)}, u32[]{:S(2)}) %collective-permute-start.8) | collective-permute-done | bytes 2097184 | tf_op jit(solution)/shard_map/ppermute | solution.py:10
  411.0 12.0 %collective-permute-done.15 = f32[2048,256]{1,0:T(8,128)S(1)} collective-permute-done((f32[2048,256]{1,0:T(8,128)}, f32[2048,256]{1,0:T(8,128)S(1)}, u32[]{:S(2)}, u32[]{:S(2)}) %collective-permute-start.15) | collective-permute-done | bytes 2097184 | tf_op jit(solution)/shard_map/ppermute | solution.py:10
  423.0 11.5 %fusion = f32[256,256]{0,1:T(8,128)S(1)} fusion(f32[128,4096]{1,0:T(8,128)} %maximum_select_fusion.4, f32[128,4096]{1,0:T(8,128)} %collective-permute-done.8, f32[2048,256]{1,0:T(8,128)} %maximum_select_fusion.5, f32[2048,256]{1,0:T(8,128)S(1)} %collective-permute-done.15, pred[]{:T(512)S(6)} %eq.35, pred[]{:T(512)S(6)} %eq.34), kind=kOutput, calls=%fused_computation.2 | convolution fusion | flops 3227516928 | bytes 8650754 | tf_op jit(solution)/shard_map/dot_general | solution.py:94
  434.5 4.9 collective-permute-start.16
  441.8 12.0 %collective-permute-done.17 = f32[256,512]{0,1:T(8,128)S(1)} collective-permute-done((f32[256,512]{0,1:T(8,128)S(1)}, f32[256,512]{0,1:T(8,128)S(1)}, u32[]{:S(2)}, u32[]{:S(2)}) %collective-permute-start.17) | collective-permute-done | bytes 524320 | tf_op jit(solution)/shard_map/ppermute | solution.py:10
  456.4 22.5 %collective-permute-done.18 = f32[256,1024]{0,1:T(8,128)S(1)} collective-permute-done((f32[256,1024]{0,1:T(8,128)S(1)}, f32[256,1024]{0,1:T(8,128)S(1)}, u32[]{:S(2)}, u32[]{:S(2)}) %collective-permute-start.18) | collective-permute-done | bytes 1048608 | tf_op jit(solution)/shard_map/ppermute | solution.py:10
  487.5 23.2 %collective-permute-done.20 = f32[128,2048]{1,0:T(8,128)S(1)} collective-permute-done((f32[128,2048]{1,0:T(8,128)S(1)}, f32[128,2048]{1,0:T(8,128)S(1)}, u32[]{:S(2)}, u32[]{:S(2)}) %collective-permute-start.20) | collective-permute-done | bytes 1048608 | tf_op jit(solution)/shard_map/ppermute | solution.py:10
  510.7 4.4 fusion.11
  521.7 9.6 %bitcast_subtract_fusion = f32[1024,2048]{1,0:T(8,128)} fusion(f32[1024,2048]{1,0:T(8,128)S(1)} %bitcast.24, f32[2048,256]{1,0:T(8,128)S(1)} %convolution_subtract_fusion, f32[1024,256]{1,0:T(8,128)S(1)} %copy-done), kind=kOutput, calls=%fused_computation | convolution fusion | flops 6444548096 | bytes 19922944 | tf_op jit(solution)/shard_map/dot_general | solution.py:100
  (81 shorter events, 87.4 us)
Async XLA Ops:
  0.0 521.7 %copy-start = (f32[1024,256]{1,0:T(8,128)S(1)}, f32[1024,256]{1,0:T(8,128)}, u32[]{:S(2)}) copy-start(f32[1024,256]{1,0:T(8,128)} %param.11) | copy-start | bytes 3145732
  43.4 5.4 %collective-permute-start = (f32[256,2048]{0,1:T(8,128)S(1)}, f32[256,2048]{0,1:T(8,128)}, u32[]{:S(2)}, u32[]{:S(2)}) collective-permute-start(f32[256,2048]{0,1:T(8,128)S(1)} %convolution_bitcast_fusion.3), channel_id=1, source_target_pairs={{0,1},{1,0},{2,3},{3,2},{4,5},{5,4},{6,7},{7,6},{8,9},{9,8},{10,11... | collective-permute-start | bytes 6291464 | tf_op jit(solution)/shard_map/ppermute | solution.py:10
  57.3 4.2 collective-permute-start.1
  61.8 47.7 %collective-permute-start.2 = (f32[256,2048]{1,0:T(8,128)S(1)}, f32[256,2048]{1,0:T(8,128)}, u32[]{:S(2)}, u32[]{:S(2)}) collective-permute-start(f32[256,2048]{1,0:T(8,128)S(1)} %add.38), channel_id=1, source_target_pairs={{0,2},{1,3},{2,0},{3,1},{4,6},{5,7},{6,4},{7,5},{8,10},{9,11},{10,... | collective-permute-start | bytes 6291464 | tf_op jit(solution)/shard_map/ppermute | solution.py:10
  120.0 4.8 collective-permute-start.3
  125.1 96.4 %copy-start.12 = (f32[64,1024]{1,0:T(8,128)S(1)}, f32[64,1024]{1,0:T(8,128)}, u32[]{:S(2)}) copy-start(f32[64,1024]{1,0:T(8,128)} %param.14) | copy-start | bytes 786436
  125.1 48.0 %collective-permute-start.4 = (f32[256,2048]{0,1:T(8,128)S(1)}, f32[256,2048]{0,1:T(8,128)S(1)}, u32[]{:S(2)}, u32[]{:S(2)}) collective-permute-start(f32[256,2048]{0,1:T(8,128)S(1)} %add.40), channel_id=1, source_target_pairs={{0,2},{1,3},{2,0},{3,1},{4,6},{5,7},{6,4},{7,5},{8,10},{9,11},{10,... | collective-permute-start | bytes 6291464 | tf_op jit(solution)/shard_map/ppermute | solution.py:10
  173.3 48.1 %collective-permute-start.5 = (f32[256,2048]{0,1:T(8,128)S(1)}, f32[256,2048]{0,1:T(8,128)}, u32[]{:S(2)}, u32[]{:S(2)}) collective-permute-start(f32[256,2048]{0,1:T(8,128)S(1)} %add.41), channel_id=1, source_target_pairs={{0,4},{1,5},{2,6},{3,7},{4,0},{5,1},{6,2},{7,3},{8,12},{9,13},{10,... | collective-permute-start | bytes 6291464 | tf_op jit(solution)/shard_map/ppermute | solution.py:10
  229.4 5.6 %collective-permute-start.9 = (f32[256,2048]{1,0:T(8,128)S(1)}, f32[256,2048]{1,0:T(8,128)S(1)}, u32[]{:S(2)}, u32[]{:S(2)}) collective-permute-start(f32[256,2048]{1,0:T(8,128)S(1)} %convolution_bitcast_fusion.1), channel_id=1, source_target_pairs={{0,1},{1,0},{2,3},{3,2},{4,5},{5,4},{6,7},{7,6},{8,9},{9,8},{10,11... | collective-permute-start | bytes 6291464 | tf_op jit(solution)/shard_map/ppermute | solution.py:10
  235.3 46.9 %collective-permute-start.10 = (f32[256,2048]{1,0:T(8,128)S(1)}, f32[256,2048]{1,0:T(8,128)S(1)}, u32[]{:S(2)}, u32[]{:S(2)}) collective-permute-start(f32[256,2048]{1,0:T(8,128)S(1)} %add.43), channel_id=1, source_target_pairs={{0,2},{1,3},{2,0},{3,1},{4,6},{5,7},{6,4},{7,5},{8,10},{9,11},{10,... | collective-permute-start | bytes 6291464 | tf_op jit(solution)/shard_map/ppermute | solution.py:10
  282.5 47.6 %collective-permute-start.11 = (f32[256,2048]{1,0:T(8,128)S(1)}, f32[256,2048]{1,0:T(8,128)}, u32[]{:S(2)}, u32[]{:S(2)}) collective-permute-start(f32[256,2048]{1,0:T(8,128)S(1)} %add.44), channel_id=1, source_target_pairs={{0,4},{1,5},{2,6},{3,7},{4,0},{5,1},{6,2},{7,3},{8,12},{9,13},{10,... | collective-permute-start | bytes 6291464 | tf_op jit(solution)/shard_map/ppermute | solution.py:10
  285.1 54.9 %collective-permute-start.6 = (f32[32,4096]{1,0:T(8,128)}, f32[32,4096]{1,0:T(8,128)}, u32[]{:S(2)}, u32[]{:S(2)}) collective-permute-start(f32[32,4096]{1,0:T(8,128)} %param.15), channel_id=1, source_target_pairs={{0,1},{1,0},{2,3},{3,2},{4,5},{5,4},{6,7},{7,6},{8,9},{9,8},{10,11... | collective-permute-start | bytes 1572872 | tf_op jit(solution)/shard_map/ppermute | solution.py:10
  331.1 5.8 %collective-permute-start.12 = (f32[256,256]{1,0:T(8,128)S(1)}, f32[256,256]{1,0:T(8,128)S(1)}, u32[]{:S(2)}, u32[]{:S(2)}) collective-permute-start(f32[256,256]{1,0:T(8,128)S(1)} %dynamic-slice_add_fusion), channel_id=1, source_target_pairs={{0,8},{1,9},{2,10},{3,11},{4,12},{5,13},{6,14},{7,15},{8,0},{9,1},... | collective-permute-start | bytes 786440 | tf_op jit(solution)/shard_map/ppermute | solution.py:10
  337.0 13.6 %collective-permute-start.13 = (f32[512,256]{1,0:T(8,128)S(1)}, f32[512,256]{1,0:T(8,128)}, u32[]{:S(2)}, u32[]{:S(2)}) collective-permute-start(f32[512,256]{1,0:T(8,128)S(1)} %maximum_select_fusion.16), channel_id=1, source_target_pairs={{0,16},{1,17},{2,18},{3,19},{4,20},{5,21},{6,22},{7,23},{8,24},{9,... | collective-permute-start | bytes 1572872 | tf_op jit(solution)/shard_map/ppermute | solution.py:10
  341.6 21.5 %collective-permute-start.7 = (f32[64,4096]{1,0:T(8,128)S(1)}, f32[64,4096]{1,0:T(8,128)}, u32[]{:S(2)}, u32[]{:S(2)}) collective-permute-start(f32[64,4096]{1,0:T(8,128)S(1)} %maximum_select_fusion.12), channel_id=1, source_target_pairs={{0,2},{1,3},{2,0},{3,1},{4,6},{5,7},{6,4},{7,5},{8,10},{9,11},{10,... | collective-permute-start | bytes 3145736 | tf_op jit(solution)/shard_map/ppermute | solution.py:10
  352.3 22.0 %collective-permute-start.14 = (f32[1024,256]{1,0:T(8,128)S(1)}, f32[1024,256]{1,0:T(8,128)}, u32[]{:S(2)}, u32[]{:S(2)}) collective-permute-start(f32[1024,256]{1,0:T(8,128)S(1)} %maximum_select_fusion.13), channel_id=1, source_target_pairs={{0,32},{1,33},{2,34},{3,35},{4,36},{5,37},{6,38},{7,39},{8,40},{9,... | collective-permute-start | bytes 3145736 | tf_op jit(solution)/shard_map/ppermute | solution.py:10
  366.3 44.7 %collective-permute-start.8 = (f32[128,4096]{1,0:T(8,128)}, f32[128,4096]{1,0:T(8,128)}, u32[]{:S(2)}, u32[]{:S(2)}) collective-permute-start(f32[128,4096]{1,0:T(8,128)} %maximum_select_fusion.4), channel_id=1, source_target_pairs={{0,4},{1,5},{2,6},{3,7},{4,0},{5,1},{6,2},{7,3},{8,12},{9,13},{10,... | collective-permute-start | bytes 6291464 | tf_op jit(solution)/shard_map/ppermute | solution.py:10
  377.5 45.4 %collective-permute-start.15 = (f32[2048,256]{1,0:T(8,128)}, f32[2048,256]{1,0:T(8,128)S(1)}, u32[]{:S(2)}, u32[]{:S(2)}) collective-permute-start(f32[2048,256]{1,0:T(8,128)} %maximum_select_fusion.5), channel_id=1, source_target_pairs={{0,64},{1,65},{2,66},{3,67},{4,68},{5,69},{6,70},{7,71},{8,72},{9,... | collective-permute-start | bytes 6291464 | tf_op jit(solution)/shard_map/ppermute | solution.py:10
  434.5 6.0 %collective-permute-start.16 = (f32[256,256]{0,1:T(8,128)S(1)}, f32[256,256]{0,1:T(8,128)S(1)}, u32[]{:S(2)}, u32[]{:S(2)}) collective-permute-start(f32[256,256]{0,1:T(8,128)S(1)} %fusion), channel_id=1, source_target_pairs={{0,1},{1,0},{2,3},{3,2},{4,5},{5,4},{6,7},{7,6},{8,9},{9,8},{10,11... | collective-permute-start | bytes 786440 | tf_op jit(solution)/shard_map/ppermute | solution.py:10
  440.6 13.2 %collective-permute-start.17 = (f32[256,512]{0,1:T(8,128)S(1)}, f32[256,512]{0,1:T(8,128)S(1)}, u32[]{:S(2)}, u32[]{:S(2)}) collective-permute-start(f32[256,512]{0,1:T(8,128)S(1)} %maximum_select_fusion.17), channel_id=1, source_target_pairs={{0,2},{1,3},{2,0},{3,1},{4,6},{5,7},{6,4},{7,5},{8,10},{9,11},{10,... | collective-permute-start | bytes 1572872 | tf_op jit(solution)/shard_map/ppermute | solution.py:10
  453.9 25.0 %collective-permute-start.18 = (f32[256,1024]{0,1:T(8,128)S(1)}, f32[256,1024]{0,1:T(8,128)S(1)}, u32[]{:S(2)}, u32[]{:S(2)}) collective-permute-start(f32[256,1024]{0,1:T(8,128)S(1)} %maximum_select_fusion.14), channel_id=1, source_target_pairs={{0,4},{1,5},{2,6},{3,7},{4,0},{5,1},{6,2},{7,3},{8,12},{9,13},{10,... | collective-permute-start | bytes 3145736 | tf_op jit(solution)/shard_map/ppermute | solution.py:10
  482.2 3.7 collective-permute-start.19
  486.0 24.7 %collective-permute-start.20 = (f32[128,2048]{1,0:T(8,128)S(1)}, f32[128,2048]{1,0:T(8,128)S(1)}, u32[]{:S(2)}, u32[]{:S(2)}) collective-permute-start(f32[128,2048]{1,0:T(8,128)S(1)} %maximum_select_fusion.15), channel_id=1, source_target_pairs={{0,2},{1,3},{2,0},{3,1},{4,6},{5,7},{6,4},{7,5},{8,10},{9,11},{10,... | collective-permute-start | bytes 3145736 | tf_op jit(solution)/shard_map/ppermute | solution.py:10
  515.2 3.6 collective-permute-start.21
  (13 other events, 299.9 us)
where the time goes:
time: 536 us; the launch traced here: 532 us
  waiting for transfers between devices  373 us (70%)
  matrix products  102 us (19%)
  starting transfers between devices  43.2 us (8%)
  other arithmetic  12.4 us (2%)
    ppermute x22, waiting for transfers between devices, partner_2(): lax.ppermute(value, axis, [(i, i ^ 1 << bit) for i in range(lax.axis_size...  373 us
    ppermute x22, starting transfers between devices, partner_2(): lax.ppermute(value, axis, [(i, i ^ 1 << bit) for i in range(lax.axis_size...  43.2 us
    dot_general x1, matrix products, shards(): solved = jnp.dot(leaf_inverse, shots, precision=highest)  29.9 us
    dot_general x1, matrix products, shards(): reduced = jnp.dot(leaf_basis, solved, precision=highest)  13.4 us
    dot_general x3, matrix products, shards(): jnp.dot(factors[:, low_rank:2 * low_rank], upper_child, precision=highest)  11.8 us
    dot_general x1, matrix products, shards(): solved_piece = jnp.dot(node_inverse, all_pieces, precision=highest)  11.5 us
  transfers between devices with their start and end apart: 22, of which 21 were waited for; matrix products, arithmetic and copies ran while one was open for 2% of the time, Pallas kernels for 0%

commit v1 on v0

v1 whole, which is shorter than its diff:
```python
import functools

import jax
import jax.numpy as jnp
from jax import lax
from jax.experimental import pallas as pl
from jax.experimental.pallas import tpu as pltpu
from jax.sharding import PartitionSpec as P

CORE, X_NEAR, X_FAR = 1, 2, 6
RINGS = (8, 32, 24, 96)
BLOCKS = 8
TREE = 8


def swap(value, mask):
    return lax.ppermute(value, "leaf", [(i, i ^ mask) for i in range(lax.axis_size("leaf"))])


def dot(a, b):
    return jnp.dot(a, b, precision=lax.Precision.HIGH)


def dot_rows(a, b):
    return lax.dot_general(a, b, (((0,), (0,)), ((), ())), precision=lax.Precision.HIGH)


def halves(value):
    high = value.astype(jnp.bfloat16)
    return high, (value - high.astype(jnp.float32)).astype(jnp.bfloat16)


def product(a_high, a_low, b_high, b_low):
    part = functools.partial(jnp.dot, preferred_element_type=jnp.float32)
    return part(a_high, b_high) + (part(a_high, b_low) + part(a_low, b_high))


def call(body, grid, in_specs, out_specs, out_shape, scratch, flops, moved):
    return pl.pallas_call(
        body,
        grid_spec=pltpu.PrefetchScalarGridSpec(
            num_scalar_prefetch=1,
            grid=grid,
            in_specs=in_specs,
            out_specs=out_specs,
            scratch_shapes=scratch,
        ),
        out_shape=out_shape,
        compiler_params=pltpu.CompilerParams(vmem_limit_bytes=40 * 2**20),
        cost_estimate=pl.CostEstimate(flops=flops, bytes_accessed=moved, transcendentals=0),
    )


def reduce_body(base, basis, inverse, shots, out, high, low):
    @pl.when(pl.program_id(0) == 0)
    def _():
        high[...], low[...] = halves(product(*halves(basis[...]), *halves(inverse[...])))

    out[...] = product(high[...], low[...], *halves(shots[...]))


def reduce_leaf(base, basis, inverse, shots):
    rank, rows = basis.shape
    width = shots.shape[1] // BLOCKS
    return call(
        reduce_body,
        (BLOCKS,),
        [
            pl.BlockSpec((rank, rows), lambda p, base: (0, 0)),
            pl.BlockSpec((rows, rows), lambda p, base: (0, 0)),
            pl.BlockSpec((rows, width), lambda p, base: (0, base[0] ^ p)),
        ],
        pl.BlockSpec((rank, width), lambda p, base: (0, p)),
        jax.ShapeDtypeStruct((rank, shots.shape[1]), jnp.float32),
        [pltpu.VMEM((rank, rows), jnp.bfloat16), pltpu.VMEM((rank, rows), jnp.bfloat16)],
        6 * rank * rows * (rows + shots.shape[1]),
        4 * (rows * rows + rows * shots.shape[1]),
    )(base, basis, inverse, shots)


def leaf_body(base, inverse, shots, out, high, low):
    @pl.when(pl.program_id(0) == 0)
    def _():
        high[...], low[...] = halves(inverse[...])

    out[...] = product(high[...], low[...], *halves(shots[...]))


def solve_leaf(base, inverse, shots, first, count):
    rows = inverse.shape[0]
    width = shots.shape[1] // BLOCKS
    return call(
        leaf_body,
        (count,),
        [
            pl.BlockSpec((rows, rows), lambda p, base: (0, 0)),
            pl.BlockSpec((rows, width), lambda p, base: (0, base[0] ^ (p + first))),
        ],
        pl.BlockSpec((rows, width), lambda p, base: (0, p)),
        jax.ShapeDtypeStruct((rows, count * width), jnp.float32),
        [pltpu.VMEM((rows, rows), jnp.bfloat16), pltpu.VMEM((rows, rows), jnp.bfloat16)],
        6 * rows * rows * count * width,
        4 * (rows * rows + 2 * rows * count * width),
    )(base, inverse, shots)


def finish_body(base, back, own, other, near, far, out, high, low):
    p = pl.program_id(0)
    half = pl.num_programs(0) // 2

    @pl.when(p == 0)
    def _():
        high[...], low[...] = halves(back[...])

    @pl.when(p < half)
    def _():
        out[...] = near[...] - product(high[...], low[...], *halves(own[...]))

    @pl.when(p >= half)
    def _():
        out[...] = far[...] - product(high[...], low[...], *halves(other[...]))


def finish(base, back, own, other, near, far):
    rows, rank = back.shape
    half = BLOCKS // 2
    width = own.shape[1] // half
    first = lambda p, base: (0, jnp.minimum(p, half - 1))
    second = lambda p, base: (0, jnp.maximum(p - half, 0))
    return call(
        finish_body,
        (BLOCKS,),
        [
            pl.BlockSpec((rows, rank), lambda p, base: (0, 0)),
            pl.BlockSpec((rank, width), first),
            pl.BlockSpec((rank, width), second),
            pl.BlockSpec((rows, width), first),
            pl.BlockSpec((rows, width), second),
        ],
        pl.BlockSpec((rows, width), lambda p, base: (0, base[0] ^ p)),
        jax.ShapeDtypeStruct((rows, BLOCKS * width), jnp.float32),
        [pltpu.VMEM((rows, rank), jnp.bfloat16), pltpu.VMEM((rows, rank), jnp.bfloat16)],
        6 * rows * rank * BLOCKS * width,
        4 * 2 * rows * BLOCKS * width,
    )(base, back, own, other, near, far)


def top_body(places, node, inverse, *rest):
    pieces, (out, high, low) = rest[:-3], rest[-3:]
    rows, width = pieces[0].shape
    for piece, (row, column, nodes) in zip(pieces, places):
        for at, mask in enumerate(nodes):
            start = pl.multiple_of((node[0] ^ mask) * 2 * rows + row * rows, rows)
            part = halves(piece[at * rows : (at + 1) * rows, :])
            high[pl.ds(start, rows), column * width : (column + 1) * width] = part[0]
            low[pl.ds(start, rows), column * width : (column + 1) * width] = part[1]
    out[...] = product(*halves(inverse[...]), high[...], low[...])


def solve_top(node, inverse, pieces, places):
    rank, order = inverse.shape
    width = 2 * pieces[0].shape[1]
    whole = lambda value: pl.BlockSpec(value.shape, lambda p, node: (0, 0))
    return call(
        functools.partial(top_body, places),
        (1,),
        [whole(inverse)] + [whole(piece) for piece in pieces],
        pl.BlockSpec((rank, width), lambda p, node: (0, 0)),
        jax.ShapeDtypeStruct((rank, width), jnp.float32),
        [pltpu.VMEM((order, width), jnp.bfloat16), pltpu.VMEM((order, width), jnp.bfloat16)],
        6 * rank * order * width,
        4 * order * (rank + width),
    )(node, inverse, *pieces)


def spread_top(reduced):
    rows, width = reduced.shape[0] // 2, reduced.shape[1] // 2
    held, order = [], [[0] for _ in RINGS]
    for quarter in range(len(RINGS)):
        row, column = divmod(quarter, 2)
        held.append([reduced[row * rows : (row + 1) * rows, column * width : (column + 1) * width]])
    for step in range(len(RINGS)):
        ways = [RINGS[(quarter + step) % len(RINGS)] for quarter in range(len(RINGS))]
        sent = [jnp.concatenate(parts, 0) if step else parts[0] for parts in held]
        arrived = [swap(value, way) for value, way in zip(sent, ways)]
        for quarter, way in enumerate(ways):
            held[quarter].append(arrived[quarter])
            order[quarter] += [mask ^ way for mask in order[quarter]]
    pieces, places = [], []
    for quarter, parts in enumerate(held):
        row, column = divmod(quarter, 2)
        at = 0
        for part in parts:
            count = part.shape[0] // rows
            pieces.append(part)
            places.append((row, column, [mask // TREE for mask in order[quarter][at : at + count]]))
            at += count
    return pieces, places


def own_first(value, second, axis):
    size = value.shape[axis] // 2
    low, high = jnp.split(value, 2, axis)
    return jnp.concatenate([jnp.where(second, high, low), jnp.where(second, low, high)], axis)


def node_blocks(factors, second, rank):
    inverse = own_first(factors[:, : 2 * rank], second, 1)
    return inverse, dot_rows(factors[:, 2 * rank : 3 * rank], inverse), factors[:, 3 * rank :]


def shards(
    shots, leaf_inverse, leaf_basis, leaf_back, level_one, level_two, level_three, top_inverse
):
    rank = leaf_basis.shape[0]
    place = lax.axis_index("leaf")
    core, near, far = place & 1, place >> 1 & 1, place >> 2 & 1
    base = jnp.reshape(core << 2 | (near ^ far) << 1 | far, (1,)).astype(jnp.int32)
    node = jnp.reshape(place // TREE, (1,)).astype(jnp.int32)
    groups = [list(range(i, i + TREE)) for i in range(0, lax.axis_size("leaf"), TREE)]
    gather = functools.partial(
        lax.all_gather, axis_name="leaf", axis_index_groups=groups, axis=0, tiled=True
    )

    three = own_first(gather(level_three), far == 1, 0)
    top_rows = gather(top_inverse)
    two_beside = swap(level_two, X_NEAR)
    one = jnp.concatenate([level_one, swap(level_one, CORE)], 0)
    two_own = jnp.concatenate([level_two, two_beside], 1)
    two_other = swap(two_own, CORE)
    two = jnp.where(
        core == 1,
        jnp.concatenate([two_other, two_own], 0),
        jnp.concatenate([two_own, two_other], 0),
    )
    two = jnp.concatenate(jnp.split(two, 2, 1), 0)
    inverse_1, down_1, back_1 = node_blocks(one, core == 1, rank)
    inverse_2, down_2, back_2 = node_blocks(two, near == 1, rank)
    inverse_3, down_3, back_3 = node_blocks(three, far == 1, rank)

    reduced = reduce_leaf(base, leaf_basis, leaf_inverse, shots)
    size = reduced.shape[1] // 2
    pair = jnp.concatenate([reduced[:, :size], swap(reduced[:, size:], CORE)], 0)
    reduced = dot(down_1, pair)
    coupled_1 = dot(inverse_1, pair)
    size //= 2
    pair = jnp.concatenate([reduced[:, :size], swap(reduced[:, size:], X_NEAR)], 0)
    reduced = dot(down_2, pair)
    coupled_2 = dot(inverse_2, pair)
    size //= 2
    pair = jnp.concatenate([reduced[:, :size], swap(reduced[:, size:], X_FAR)], 0)
    reduced = dot(down_3, pair)
    coupled_3 = dot(inverse_3, pair)

    solved_near = solve_leaf(base, leaf_inverse, shots, 0, BLOCKS // 2)
    solved_far = solve_leaf(base, leaf_inverse, shots, BLOCKS // 2, BLOCKS // 2)

    pieces, places = spread_top(reduced)
    coefficient = solve_top(node, top_rows, pieces, places)
    for coupled, back, mask in ((coupled_3, back_3, X_FAR), (coupled_2, back_2, X_NEAR)):
        other = swap(coupled[rank:] - dot(back[rank:], coefficient), mask)
        own = coupled[:rank] - dot(back[:rank], coefficient)
        coefficient = jnp.concatenate([own, other], 1)
    other = swap(coupled_1[rank:] - dot(back_1[rank:], coefficient), CORE)
    own = coupled_1[:rank] - dot(back_1[:rank], coefficient)
    return finish(base, leaf_back, own, other, solved_near, solved_far)


def solution(mesh):
    return jax.shard_map(
        shards,
        mesh=mesh,
        in_specs=(P("leaf", None),) * 8,
        out_specs=P("leaf", None),
        check_vma=False,
    )
```

time: 536 us -> 170 us (0.32)
  waiting for transfers between devices: 373 us -> 30.8 us
  matrix products: 102 us -> 18.6 us
  Pallas kernels: 0 us -> 40.4 us
  local copies, waits for them, and re-layouts: 0.07 us -> 14.8 us
  between operations: 0.6 us -> 14.1 us
  other arithmetic: 12.4 us -> 6.04 us
    ppermute x22 -> x25, waiting for transfers between devices: 373 us -> 29.4 us  [swap(): lax.ppermute(value, 'leaf', [(i, i ^ mask) for i in range(lax.axis_size('...]
    dot_general x16 -> x15, matrix products: 102 us -> 18.6 us  [the longest x12 16.7 us: dot(): return jnp.dot(a, b, precision=lax.Precision.HIGH)]
    pallas_call x0 -> x5, Pallas kernels: none -> 40.4 us  [the longest x2 18.9 us: solve_leaf(): call(leaf_body, (count,), [pl.BlockSpec((rows, rows), lambda p, base: (0,...]
    unnamed x30 -> x60, local copies, waits for them, and re-layouts: 0.07 us -> 10.9 us
    select_n x8 -> x7, other arithmetic: 10 us -> 2.59 us  [the longest x4 2.19 us: own_first(): jnp.where(second, high, low)]
    ppermute x22 -> x25, starting transfers between devices: 43.2 us -> 44.2 us  [swap(): lax.ppermute(value, 'leaf', [(i, i ^ mask) for i in range(lax.axis_size('...]
  transfers between devices with their start and end apart: 22 -> 27, of which waited for: 21 -> 11; matrix products, arithmetic and copies ran while one was open for 2% -> 14% of each run, Pallas kernels for 0% -> 17%
where the time goes in v1:
time: 170 us; the launch traced here: 169 us
  starting transfers between devices  44.3 us (26%)
  Pallas kernels  40.4 us (24%)
  waiting for transfers between devices  30.8 us (18%)
  matrix products  18.6 us (11%)
  local copies, waits for them, and re-layouts  14.8 us (9%)
  between operations  14.1 us (8%)
  other arithmetic  6.04 us (4%)
    ppermute x25, starting transfers between devices, swap(): lax.ppermute(value, 'leaf', [(i, i ^ mask) for i in range(lax.axis_size('...  44.2 us
    ppermute x25, waiting for transfers between devices, swap(): lax.ppermute(value, 'leaf', [(i, i ^ mask) for i in range(lax.axis_size('...  29.4 us
    pallas_call x2, Pallas kernels, solve_leaf(): call(leaf_body, (count,), [pl.BlockSpec((rows, rows), lambda p, base: (0,...  18.9 us
    dot_general x12, matrix products, dot(): return jnp.dot(a, b, precision=lax.Precision.HIGH)  16.7 us
    unnamed x60, local copies, waits for them, and re-layouts  10.9 us
    pallas_call x1, Pallas kernels, reduce_leaf(): call(reduce_body, (BLOCKS,), [pl.BlockSpec((rank, rows), lambda p, base:...  9.99 us
    pallas_call x1, Pallas kernels, finish(): call(finish_body, (BLOCKS,), [pl.BlockSpec((rows, rank), lambda p, base:...  7.67 us
    pallas_call x1, Pallas kernels, solve_top(): call(functools.partial(top_body, places), (1,), [whole(inverse)] + [whole...  3.82 us
  transfers between devices with their start and end apart: 27, of which 11 were waited for; matrix products, arithmetic and copies ran while one was open for 14% of the time, Pallas kernels for 17%

profile of v1, /device:TPU:1, one launch (start us, length us, event | category | flops | bytes accessed | tf_op | source)
XLA Modules:
  0.0 169.0 jit_solution(7837991455790515689)
XLA Ops:
  8.0 2.1 %collective-permute-start.2 = (f32[128,1024]{1,0:T(8,128)}, f32[128,1024]{1,0:T(8,128)}, u32[]{:S(2)}, u32[]{:S(2)}) collective-permute-start(f32[128,1024]{1,0:T(8,128)} %param.13), channel_id=1, source_target_pairs={{0,2},{1,3},{2,0},{3,1},{4,6},{5,7},{6,4},{7,5},{8,10},{9,11},{10,... | collective-permute-start | bytes 1572872 | tf_op jit(solution)/shard_map/ppermute | solution.py:17
  11.1 2.2 %copy-done.2 = f32[1024,1024]{1,0:T(8,128)S(1)} copy-done((f32[1024,1024]{1,0:T(8,128)S(1)}, f32[1024,1024]{1,0:T(8,128)}, u32[]{:S(2)}) %copy-start.2) | copy-done | bytes 4194328
  14.5 10.0 %shard_map.82 = f32[256,2048]{1,0:T(8,128)S(1)} custom-call(s32[1]{0:T(128)} %bitcast.base, f32[256,1024]{1,0:T(8,128)S(1)} %copy-done.4, f32[1024,1024]{1,0:T(8,128)S(1)} %copy-done.2, f32[1024,2048]{1,0:T(8,128)} %shots.5), custom_call_target="tpu_custom_call" | custom-call | flops 4831838208 | bytes 12582912 | tf_op jit(solution)/shard_map/pallas_call | solution.py:65
  35.4 10.6 %collective-permute-done.4 = f32[256,512]{1,0:T(8,128)S(1)} collective-permute-done((f32[256,512]{1,0:T(8,128)S(1)}, f32[256,512]{1,0:T(8,128)S(1)}, u32[]{:S(2)}, u32[]{:S(2)}) %collective-permute-start.4) | collective-permute-done | bytes 524320 | tf_op jit(solution)/shard_map/ppermute | solution.py:17
  48.4 1.9 %slice_select_fusion.1 = (f32[256,1024]{1,0:T(8,128)S(1)}, f32[256,1024]{1,0:T(8,128)S(1)}) fusion(f32[512,1024]{1,0:T(8,128)} %all-gather.3.cloned.1.call-done, pred[]{:T(512)S(6)} %eq.13), kind=kLoop, calls=%fused_computation.14 | loop fusion | flops 524288 | bytes 4194305 | tf_op jit(solution)/shard_map/jit(_where)/select_n | solution.py:204
  52.3 3.8 %collective-permute-done.5 = f32[256,256]{1,0:T(8,128)S(1)} collective-permute-done((f32[256,256]{1,0:T(8,128)S(1)}, f32[256,256]{1,0:T(8,128)S(1)}, u32[]{:S(2)}, u32[]{:S(2)}) %collective-permute-start.5) | collective-permute-done | bytes 262176 | tf_op jit(solution)/shard_map/ppermute | solution.py:17
  57.3 6.4 %collective-permute-start.18 = (f32[128,128]{1,0:T(8,128)S(1)}, f32[128,128]{1,0:T(8,128)S(1)}, u32[]{:S(2)}, u32[]{:S(2)}) collective-permute-start(f32[128,128]{1,0:T(8,128)S(1)} %get-tuple-element.25.rest_15_), channel_id=1, source_target_pairs={{0,96},{1,97},{2,98},{3,99},{4,100},{5,101},{6,102},{7,103},{8,104... | collective-permute-start | bytes 196616 | tf_op jit(solution)/shard_map/ppermute | solution.py:17
  63.7 3.5 %collective-permute-start.14 = (f32[128,128]{1,0:T(8,128)S(1)}, f32[128,128]{1,0:T(8,128)S(1)}, u32[]{:S(2)}, u32[]{:S(2)}) collective-permute-start(f32[128,128]{1,0:T(8,128)S(1)} %get-tuple-element.26.rest_10_), channel_id=1, source_target_pairs={{0,24},{1,25},{2,26},{3,27},{4,28},{5,29},{6,30},{7,31},{8,16},{9,... | collective-permute-start | bytes 196616 | tf_op jit(solution)/shard_map/ppermute | solution.py:17
  70.7 1.7 %collective-permute-start.11 = (f32[256,128]{1,0:T(8,128)S(1)}, f32[256,128]{1,0:T(8,128)S(1)}, u32[]{:S(2)}, u32[]{:S(2)}) collective-permute-start(f32[256,128]{1,0:T(8,128)S(1)} %pad_maximum_fusion.49), channel_id=1, source_target_pairs={{0,24},{1,25},{2,26},{3,27},{4,28},{5,29},{6,30},{7,31},{8,16},{9,... | collective-permute-start | bytes 393224 | tf_op jit(solution)/shard_map/ppermute | solution.py:17
  77.3 2.8 %collective-permute-start.8 = (f32[512,128]{1,0:T(8,128)S(1)}, f32[512,128]{1,0:T(8,128)S(1)}, u32[]{:S(2)}, u32[]{:S(2)}) collective-permute-start(f32[512,128]{1,0:T(8,128)S(1)} %pad_maximum_fusion.44), channel_id=1, source_target_pairs={{0,24},{1,25},{2,26},{3,27},{4,28},{5,29},{6,30},{7,31},{8,16},{9,... | collective-permute-start | bytes 786440 | tf_op jit(solution)/shard_map/ppermute | solution.py:17
  84.6 1.8 %collective-permute-start.9 = (f32[1024,128]{1,0:T(8,128)}, f32[1024,128]{1,0:T(8,128)}, u32[]{:S(2)}, u32[]{:S(2)}) collective-permute-start(f32[1024,128]{1,0:T(8,128)} %pad_maximum_fusion.31), channel_id=1, source_target_pairs={{0,96},{1,97},{2,98},{3,99},{4,100},{5,101},{6,102},{7,103},{8,104... | collective-permute-start | bytes 1572872 | tf_op jit(solution)/shard_map/ppermute | solution.py:17
  86.4 2.7 %fusion.3 = f32[512,256]{0,1:T(8,128)} fusion(f32[512,256]{1,0:T(8,128)} %copy-done.16, f32[512,256]{1,0:T(8,128)} %copy-done.19, f32[256,256]{1,0:T(8,128)} %copy-done.28, f32[256,256]{1,0:T(8,128)S(1)} %get-tuple-element.23), kind=kOutput, calls=%fused_computation.16 | convolution fusion | flops 403046400 | bytes 2097152 | tf_op jit(solution)/shard_map/dot_general | solution.py:21
  89.1 4.9 %collective-permute-done.21.rest_19_ = f32[1024,128]{1,0:T(8,128)S(1)} collective-permute-done((f32[1024,128]{1,0:T(8,128)}, f32[1024,128]{1,0:T(8,128)S(1)}, u32[]{:S(2)}, u32[]{:S(2)}) %collective-permute-start.21) | collective-permute-done | bytes 524320 | tf_op jit(solution)/shard_map/ppermute | solution.py:17
  94.4 2.2 %copy-done = f32[256,4096]{1,0:T(8,128)S(1)} copy-done((f32[256,4096]{1,0:T(8,128)S(1)}, f32[256,4096]{1,0:T(8,128)}, u32[]{:S(2)}) %copy-start) | copy-done | bytes 4194328
  96.6 3.8 %shard_map.83 = f32[256,256]{1,0:T(8,128)S(1)} custom-call(s32[1]{0:T(128)} %bitcast.1.node, f32[256,4096]{1,0:T(8,128)S(1)} %copy-done, f32[128,128]{1,0:T(8,128)S(1)} %get-tuple-element.28.rest_0_, f32[128,128]{1,0:T(8,128)S(1)} %collective-permute-done.6.rest_1_, f32[256,128]{1,0:T(8,128)S(1)} %collective-permute-done.7.rest_2_, ...), custom_call_target="tpu_custom_call" | custom-call | flops 1610612736 | bytes 8388608 | tf_op jit(solution)/shard_map/pallas_call | solution.py:164
  103.3 5.0 %collective-permute-start.22 = (f32[256,256]{0,1:T(8,128)S(1)}, f32[256,256]{0,1:T(8,128)S(1)}, u32[]{:S(2)}, u32[]{:S(2)}) collective-permute-start(f32[256,256]{0,1:T(8,128)S(1)} %get-tuple-element.22), channel_id=1, source_target_pairs={{0,6},{1,7},{2,4},{3,5},{4,2},{5,3},{6,0},{7,1},{8,14},{9,15},{10,... | collective-permute-start | bytes 786440 | tf_op jit(solution)/shard_map/ppermute | solution.py:17
  109.3 2.7 %collective-permute-done.22 = f32[256,256]{0,1:T(8,128)S(1)} collective-permute-done((f32[256,256]{0,1:T(8,128)S(1)}, f32[256,256]{0,1:T(8,128)S(1)}, u32[]{:S(2)}, u32[]{:S(2)}) %collective-permute-start.22) | collective-permute-done | bytes 262176 | tf_op jit(solution)/shard_map/ppermute | solution.py:17
  113.6 1.9 %fusion.1 = f32[512,1024]{1,0:T(8,128)S(1)} fusion(f32[256,1024]{1,0:T(8,128)S(1)} %copy-done.23, f32[256,1024]{1,0:T(8,128)S(1)} %copy-done.9, f32[512,256]{1,0:T(8,128)S(1)} %copy-done.13, f32[512,256]{1,0:T(8,128)S(1)} %copy-done.11), kind=kOutput, calls=%fused_computation.3 | convolution fusion | flops 1611399168 | bytes 5242880 | tf_op jit(solution)/shard_map/dot_general | solution.py:21
  117.1 4.5 %collective-permute-done.23 = f32[256,512]{0,1:T(8,128)S(1)} collective-permute-done((f32[256,512]{0,1:T(8,128)S(1)}, f32[256,512]{0,1:T(8,128)S(1)}, u32[]{:S(2)}, u32[]{:S(2)}) %collective-permute-start.23) | collective-permute-done | bytes 524320 | tf_op jit(solution)/shard_map/ppermute | solution.py:17
  123.1 10.7 %collective-permute-start.24 = (f32[256,1024]{1,0:T(8,128)S(1)}, f32[256,1024]{1,0:T(8,128)S(1)}, u32[]{:S(2)}, u32[]{:S(2)}) collective-permute-start(f32[256,1024]{1,0:T(8,128)S(1)} %slice_subtract_fusion), channel_id=1, source_target_pairs={{0,1},{1,0},{2,3},{3,2},{4,5},{5,4},{6,7},{7,6},{8,9},{9,8},{10,11... | collective-permute-start | bytes 3145736 | tf_op jit(solution)/shard_map/ppermute | solution.py:17
  133.9 9.4 %shard_map.85.far = f32[1024,1024]{1,0:T(8,128)S(1)} custom-call(s32[1]{0:T(128)} %bitcast.base, f32[1024,1024]{1,0:T(8,128)S(1)} %copy-done.3, f32[1024,2048]{1,0:T(8,128)} %shots.5), custom_call_target="tpu_custom_call" | custom-call | flops 6442450944 | bytes 12582912 | tf_op jit(solution)/shard_map/pallas_call | solution.py:92
  143.3 9.5 %shard_map.84.near = f32[1024,1024]{1,0:T(8,128)S(1)} custom-call(s32[1]{0:T(128)} %bitcast.base, f32[1024,1024]{1,0:T(8,128)S(1)} %copy-done.3, f32[1024,2048]{1,0:T(8,128)} %shots.5), custom_call_target="tpu_custom_call" | custom-call | flops 6442450944 | bytes 12582912 | tf_op jit(solution)/shard_map/pallas_call | solution.py:92
  152.8 1.7 slice_subtract_fusion.1.own
  154.5 7.7 %shard_map.86 = f32[1024,2048]{1,0:T(8,128)} custom-call(s32[1]{0:T(128)} %bitcast.base, f32[1024,256]{1,0:T(8,128)S(1)} %copy-done.1, f32[256,1024]{1,0:T(8,128)S(1)} %slice_subtract_fusion.1.own, f32[256,1024]{1,0:T(8,128)S(1)} %collective-permute-done.24.other, f32[1024,1024]{1,0:T(8,128)S(1)} %shard_map.84.near, f32[1024,1024]{1,0:T(8,128)S(1)} %shard_map.85.far), custom_call_target="tpu_custom_call" | custom-call | flops 3221225472 | bytes 16777216 | tf_op jit(solution)/shard_map/pallas_call | solution.py:130
  (138 shorter events, 41.5 us)
Async XLA Ops:
  6.5 41.9 %all-gather.3.cloned.1.call-start = ((), (), s32[]{:S(2)}) async-start(), calls=%async_computation | async-start | bytes 2359296 | tf_op jit(solution)/shard_map/all_gather | solution.py:225
  7.3 87.1 %all-gather.5.cloned.1.call-start = ((), (), s32[]{:S(2)}) async-start(), calls=%async_computation.1 | async-start | bytes 4718592 | tf_op jit(solution)/shard_map/all_gather | solution.py:226
  8.0 19.2 %collective-permute-start.2 = (f32[128,1024]{1,0:T(8,128)}, f32[128,1024]{1,0:T(8,128)}, u32[]{:S(2)}, u32[]{:S(2)}) collective-permute-start(f32[128,1024]{1,0:T(8,128)} %param.13), channel_id=1, source_target_pairs={{0,2},{1,3},{2,0},{3,1},{4,6},{5,7},{6,4},{7,5},{8,10},{9,11},{10,... | collective-permute-start | bytes 1572872 | tf_op jit(solution)/shard_map/ppermute | solution.py:17
  10.1 18.4 %collective-permute-start = (f32[256,1024]{1,0:T(8,128)}, f32[256,1024]{1,0:T(8,128)}, u32[]{:S(2)}, u32[]{:S(2)}) collective-permute-start(f32[256,1024]{1,0:T(8,128)} %param.12), channel_id=1, source_target_pairs={{0,1},{1,0},{2,3},{3,2},{4,5},{5,4},{6,7},{7,6},{8,9},{9,8},{10,11... | collective-permute-start | bytes 3145736 | tf_op jit(solution)/shard_map/ppermute | solution.py:17
  25.7 5.7 %collective-permute-start.1 = (f32[256,1024]{1,0:T(8,128)}, f32[256,1024]{1,0:T(8,128)S(1)}, u32[]{:S(2)}, u32[]{:S(2)}) collective-permute-start(f32[256,1024]{1,0:T(8,128)} %get-tuple-element.18), channel_id=1, source_target_pairs={{0,1},{1,0},{2,3},{3,2},{4,5},{5,4},{6,7},{7,6},{8,9},{9,8},{10,11... | collective-permute-start | bytes 3145736 | tf_op jit(solution)/shard_map/ppermute | solution.py:17
  32.7 13.4 %collective-permute-start.4 = (f32[256,512]{1,0:T(8,128)S(1)}, f32[256,512]{1,0:T(8,128)S(1)}, u32[]{:S(2)}, u32[]{:S(2)}) collective-permute-start(f32[256,512]{1,0:T(8,128)S(1)} %get-tuple-element.20), channel_id=1, source_target_pairs={{0,2},{1,3},{2,0},{3,1},{4,6},{5,7},{6,4},{7,5},{8,10},{9,11},{10,... | collective-permute-start | bytes 1572872 | tf_op jit(solution)/shard_map/ppermute | solution.py:17
  46.8 9.3 %collective-permute-start.5 = (f32[256,256]{1,0:T(8,128)S(1)}, f32[256,256]{1,0:T(8,128)S(1)}, u32[]{:S(2)}, u32[]{:S(2)}) collective-permute-start(f32[256,256]{1,0:T(8,128)S(1)} %get-tuple-element.24), channel_id=1, source_target_pairs={{0,6},{1,7},{2,4},{3,5},{4,2},{5,3},{6,0},{7,1},{8,14},{9,15},{10,... | collective-permute-start | bytes 786440 | tf_op jit(solution)/shard_map/ppermute | solution.py:17
  57.3 9.9 %collective-permute-start.18 = (f32[128,128]{1,0:T(8,128)S(1)}, f32[128,128]{1,0:T(8,128)S(1)}, u32[]{:S(2)}, u32[]{:S(2)}) collective-permute-start(f32[128,128]{1,0:T(8,128)S(1)} %get-tuple-element.25.rest_15_), channel_id=1, source_target_pairs={{0,96},{1,97},{2,98},{3,99},{4,100},{5,101},{6,102},{7,103},{8,104... | collective-permute-start | bytes 196616 | tf_op jit(solution)/shard_map/ppermute | solution.py:17
  63.7 5.6 %collective-permute-start.14 = (f32[128,128]{1,0:T(8,128)S(1)}, f32[128,128]{1,0:T(8,128)S(1)}, u32[]{:S(2)}, u32[]{:S(2)}) collective-permute-start(f32[128,128]{1,0:T(8,128)S(1)} %get-tuple-element.26.rest_10_), channel_id=1, source_target_pairs={{0,24},{1,25},{2,26},{3,27},{4,28},{5,29},{6,30},{7,31},{8,16},{9,... | collective-permute-start | bytes 196616 | tf_op jit(solution)/shard_map/ppermute | solution.py:17
  67.2 5.2 %collective-permute-start.6 = (f32[128,128]{1,0:T(8,128)S(1)}, f32[128,128]{1,0:T(8,128)S(1)}, u32[]{:S(2)}, u32[]{:S(2)}) collective-permute-start(f32[128,128]{1,0:T(8,128)S(1)} %get-tuple-element.28.rest_0_), channel_id=1, source_target_pairs={{0,8},{1,9},{2,10},{3,11},{4,12},{5,13},{6,14},{7,15},{8,0},{9,1},... | collective-permute-start | bytes 196616 | tf_op jit(solution)/shard_map/ppermute | solution.py:17
  67.2 5.3 %collective-permute-start.19 = (f32[256,128]{1,0:T(8,128)S(1)}, f32[256,128]{1,0:T(8,128)S(1)}, u32[]{:S(2)}, u32[]{:S(2)}) collective-permute-start(f32[256,128]{1,0:T(8,128)S(1)} %pad_maximum_fusion.51), channel_id=1, source_target_pairs={{0,8},{1,9},{2,10},{3,11},{4,12},{5,13},{6,14},{7,15},{8,0},{9,1},... | collective-permute-start | bytes 393224 | tf_op jit(solution)/shard_map/ppermute | solution.py:17
  69.3 5.1 %collective-permute-start.15 = (f32[256,128]{1,0:T(8,128)S(1)}, f32[256,128]{1,0:T(8,128)S(1)}, u32[]{:S(2)}, u32[]{:S(2)}) collective-permute-start(f32[256,128]{1,0:T(8,128)S(1)} %pad_maximum_fusion.50), channel_id=1, source_target_pairs={{0,96},{1,97},{2,98},{3,99},{4,100},{5,101},{6,102},{7,103},{8,104... | collective-permute-start | bytes 393224 | tf_op jit(solution)/shard_map/ppermute | solution.py:17
  70.7 5.1 %collective-permute-start.11 = (f32[256,128]{1,0:T(8,128)S(1)}, f32[256,128]{1,0:T(8,128)S(1)}, u32[]{:S(2)}, u32[]{:S(2)}) collective-permute-start(f32[256,128]{1,0:T(8,128)S(1)} %pad_maximum_fusion.49), channel_id=1, source_target_pairs={{0,24},{1,25},{2,26},{3,27},{4,28},{5,29},{6,30},{7,31},{8,16},{9,... | collective-permute-start | bytes 393224 | tf_op jit(solution)/shard_map/ppermute | solution.py:17
  72.6 7.4 %collective-permute-start.20 = (f32[512,128]{1,0:T(8,128)S(1)}, f32[512,128]{1,0:T(8,128)S(1)}, u32[]{:S(2)}, u32[]{:S(2)}) collective-permute-start(f32[512,128]{1,0:T(8,128)S(1)} %pad_maximum_fusion.47), channel_id=1, source_target_pairs={{0,32},{1,33},{2,34},{3,35},{4,36},{5,37},{6,38},{7,39},{8,40},{9,... | collective-permute-start | bytes 786440 | tf_op jit(solution)/shard_map/ppermute | solution.py:17
  74.4 6.9 %collective-permute-start.16 = (f32[512,128]{1,0:T(8,128)S(1)}, f32[512,128]{1,0:T(8,128)S(1)}, u32[]{:S(2)}, u32[]{:S(2)}) collective-permute-start(f32[512,128]{1,0:T(8,128)S(1)} %pad_maximum_fusion.46), channel_id=1, source_target_pairs={{0,8},{1,9},{2,10},{3,11},{4,12},{5,13},{6,14},{7,15},{8,0},{9,1},... | collective-permute-start | bytes 786440 | tf_op jit(solution)/shard_map/ppermute | solution.py:17
  75.9 6.5 %collective-permute-start.12 = (f32[512,128]{1,0:T(8,128)S(1)}, f32[512,128]{1,0:T(8,128)S(1)}, u32[]{:S(2)}, u32[]{:S(2)}) collective-permute-start(f32[512,128]{1,0:T(8,128)S(1)} %pad_maximum_fusion.45), channel_id=1, source_target_pairs={{0,96},{1,97},{2,98},{3,99},{4,100},{5,101},{6,102},{7,103},{8,104... | collective-permute-start | bytes 786440 | tf_op jit(solution)/shard_map/ppermute | solution.py:17
  77.3 6.5 %collective-permute-start.8 = (f32[512,128]{1,0:T(8,128)S(1)}, f32[512,128]{1,0:T(8,128)S(1)}, u32[]{:S(2)}, u32[]{:S(2)}) collective-permute-start(f32[512,128]{1,0:T(8,128)S(1)} %pad_maximum_fusion.44), channel_id=1, source_target_pairs={{0,24},{1,25},{2,26},{3,27},{4,28},{5,29},{6,30},{7,31},{8,16},{9,... | collective-permute-start | bytes 786440 | tf_op jit(solution)/shard_map/ppermute | solution.py:17
  80.9 13.2 %collective-permute-start.21 = (f32[1024,128]{1,0:T(8,128)}, f32[1024,128]{1,0:T(8,128)S(1)}, u32[]{:S(2)}, u32[]{:S(2)}) collective-permute-start(f32[1024,128]{1,0:T(8,128)} %pad_maximum_fusion.34), channel_id=1, source_target_pairs={{0,24},{1,25},{2,26},{3,27},{4,28},{5,29},{6,30},{7,31},{8,16},{9,... | collective-permute-start | bytes 1572872 | tf_op jit(solution)/shard_map/ppermute | solution.py:17
  82.2 11.9 %collective-permute-start.17 = (f32[1024,128]{1,0:T(8,128)}, f32[1024,128]{1,0:T(8,128)S(1)}, u32[]{:S(2)}, u32[]{:S(2)}) collective-permute-start(f32[1024,128]{1,0:T(8,128)} %pad_maximum_fusion.33), channel_id=1, source_target_pairs={{0,32},{1,33},{2,34},{3,35},{4,36},{5,37},{6,38},{7,39},{8,40},{9,... | collective-permute-start | bytes 1572872 | tf_op jit(solution)/shard_map/ppermute | solution.py:17
  83.2 10.8 %collective-permute-start.13 = (f32[1024,128]{1,0:T(8,128)}, f32[1024,128]{1,0:T(8,128)}, u32[]{:S(2)}, u32[]{:S(2)}) collective-permute-start(f32[1024,128]{1,0:T(8,128)} %pad_maximum_fusion.32), channel_id=1, source_target_pairs={{0,8},{1,9},{2,10},{3,11},{4,12},{5,13},{6,14},{7,15},{8,0},{9,1},... | collective-permute-start | bytes 1572872 | tf_op jit(solution)/shard_map/ppermute | solution.py:17
  84.6 9.7 %collective-permute-start.9 = (f32[1024,128]{1,0:T(8,128)}, f32[1024,128]{1,0:T(8,128)}, u32[]{:S(2)}, u32[]{:S(2)}) collective-permute-start(f32[1024,128]{1,0:T(8,128)} %pad_maximum_fusion.31), channel_id=1, source_target_pairs={{0,96},{1,97},{2,98},{3,99},{4,100},{5,101},{6,102},{7,103},{8,104... | collective-permute-start | bytes 1572872 | tf_op jit(solution)/shard_map/ppermute | solution.py:17
  103.3 8.7 %collective-permute-start.22 = (f32[256,256]{0,1:T(8,128)S(1)}, f32[256,256]{0,1:T(8,128)S(1)}, u32[]{:S(2)}, u32[]{:S(2)}) collective-permute-start(f32[256,256]{0,1:T(8,128)S(1)} %get-tuple-element.22), channel_id=1, source_target_pairs={{0,6},{1,7},{2,4},{3,5},{4,2},{5,3},{6,0},{7,1},{8,14},{9,15},{10,... | collective-permute-start | bytes 786440 | tf_op jit(solution)/shard_map/ppermute | solution.py:17
  113.5 8.1 %collective-permute-start.23 = (f32[256,512]{0,1:T(8,128)S(1)}, f32[256,512]{0,1:T(8,128)S(1)}, u32[]{:S(2)}, u32[]{:S(2)}) collective-permute-start(f32[256,512]{0,1:T(8,128)S(1)} %slice_subtract_fusion.2), channel_id=1, source_target_pairs={{0,2},{1,3},{2,0},{3,1},{4,6},{5,7},{6,4},{7,5},{8,10},{9,11},{10,... | collective-permute-start | bytes 1572872 | tf_op jit(solution)/shard_map/ppermute | solution.py:17
  123.1 31.3 %collective-permute-start.24 = (f32[256,1024]{1,0:T(8,128)S(1)}, f32[256,1024]{1,0:T(8,128)S(1)}, u32[]{:S(2)}, u32[]{:S(2)}) collective-permute-start(f32[256,1024]{1,0:T(8,128)S(1)} %slice_subtract_fusion), channel_id=1, source_target_pairs={{0,1},{1,0},{2,3},{3,2},{4,5},{5,4},{6,7},{7,6},{8,9},{9,8},{10,11... | collective-permute-start | bytes 3145736 | tf_op jit(solution)/shard_map/ppermute | solution.py:17
  (32 other events, 168.3 us)
Sparse Core Ops, SparseCore 0:
  9.1 28.7 all-gather.2
  39.6 35.3 all-gather.4

commit v2 on v0

v2 whole, which is shorter than its diff:
```python
import functools
import math

import jax
import jax.numpy as jnp
from jax import lax
from jax.experimental import pallas as pl
from jax.experimental.pallas import tpu as pltpu
from jax.sharding import PartitionSpec as P

CORE, X_NEAR, X_FAR = 1, 2, 6
RINGS = (8, 32, 24, 96)
BLOCKS = 8
TREE = 8


def swap(value, mask):
    return lax.ppermute(value, "leaf", [(i, i ^ mask) for i in range(lax.axis_size("leaf"))])


ROW_STEPS = 4
SPARE_BYTES = 6 * 2**20


def after(values, ready):
    return lax.optimization_barrier((values, ready))[0]


def halves(value):
    high = value.astype(jnp.bfloat16)
    return high, (value - high.astype(jnp.float32)).astype(jnp.bfloat16)


part = functools.partial(jnp.dot, preferred_element_type=jnp.float32)


def product(a_high, a_low, b):
    b_high, b_low = halves(b)
    return part(a_high, b_high) + (part(a_high, b_low) + part(a_low, b_high))


def pair_product(a_high, a_low, own, other):
    rank = own.shape[0]
    return product(a_high[:, :rank], a_low[:, :rank], own) + product(
        a_high[:, rank:], a_low[:, rank:], other
    )


def call(body, grid, scalars, operands, results, scratch, flops, aliases=None):
    zero = lambda p, s: (0, 0)
    full = lambda item: item if isinstance(item, tuple) else (item, item.shape, zero)
    operands, results = [full(item) for item in operands], [full(item) for item in results]
    spec = lambda item: pl.BlockSpec(memory_space=pl.ANY) if item[1] is None else pl.BlockSpec(item[1], item[2])
    held = 2 * sum(math.prod(item[1]) * item[0].dtype.itemsize for item in operands + results if item[1])
    held += sum(math.prod(item.shape) * jnp.dtype(item.dtype).itemsize for item in scratch)
    moved = sum(4 * math.prod(item[0].shape) for item in operands + results)
    return pl.pallas_call(
        body,
        grid_spec=pltpu.PrefetchScalarGridSpec(
            num_scalar_prefetch=1,
            grid=(grid,),
            in_specs=[spec(item) for item in operands],
            out_specs=[spec(item) for item in results],
            scratch_shapes=scratch,
        ),
        out_shape=[item[0] for item in results],
        input_output_aliases=aliases or {},
        compiler_params=pltpu.CompilerParams(vmem_limit_bytes=held + SPARE_BYTES),
        cost_estimate=pl.CostEstimate(flops=flops, bytes_accessed=moved if flops else 0, transcendentals=0),
    )(scalars, *[item[0] for item in operands])


def f32(*shape):
    return jax.ShapeDtypeStruct(shape, jnp.float32)


def hbm(value):
    return pltpu.with_memory_space_constraint(value, pltpu.HBM)


def both(*shape, space=jax.ShapeDtypeStruct):
    return [space(shape, jnp.bfloat16)] * 2


def lead_body(base, basis, inverse, shots, high, low, *pieces):
    p = pl.program_id(0)

    @pl.when(p == 0)
    def _():
        high[...], low[...] = halves(product(*halves(basis[...]), inverse[...]))

    reduced = product(high[...], low[...], shots[...])
    for i, piece in enumerate(pieces):

        @pl.when(p == i)
        def _():
            piece[...] = reduced


def reduce_lead(base, basis, inverse, shots):
    rank, rows = basis.shape
    width, half = shots.shape[1] // BLOCKS, BLOCKS // 2
    return call(
        lead_body,
        half,
        base,
        [basis, hbm(inverse), (hbm(shots), (rows, width), lambda p, base: (0, base[0] ^ (p + half)))],
        both(rank, rows) + [f32(rank, width)] * half,
        [],
        6 * rank * rows * (rows + half * width),
    )


def reduce_body(base, high, low, shots, out):
    out[...] = product(high[...], low[...], shots[...])


def reduce_own(base, high, low, shots):
    rank, rows = high.shape
    width, half = shots.shape[1] // BLOCKS, BLOCKS // 2
    return call(
        reduce_body,
        half,
        base,
        [high, low, (hbm(shots), (rows, width), lambda p, base: (0, base[0] ^ p))],
        [(f32(rank, half * width), (rank, width), lambda p, base: (0, p))],
        [],
        6 * rank * rows * half * width,
    )[0]


def leaf_body(half, inverse, shots, out, high, low):
    @pl.when(pl.program_id(0) == 0)
    def _():
        high[...], low[...] = halves(shots[...])

    a_high, a_low = halves(inverse[...])
    out[...] = part(a_high, high[...]) + (part(a_high, low[...]) + part(a_low, high[...]))


def solve_leaf(half, inverse, shots, space):
    rows = inverse.shape[0]
    width, unit = shots.shape[1] // 2, rows // ROW_STEPS
    return call(
        leaf_body,
        ROW_STEPS,
        half,
        [(hbm(inverse), (unit, rows), lambda p, half: (p, 0)), (hbm(shots), (rows, width), lambda p, half: (0, half[0]))],
        [(space((rows, width), jnp.float32), (unit, width), lambda p, half: (p, 0))],
        [pltpu.VMEM((rows, width), jnp.bfloat16)] * 2,
        6 * rows * rows * width,
    )[0]


def finish_body(at, back, coefficient, solved, *rest):
    out, high, low = rest[-3:]

    @pl.when(pl.program_id(0) == 0)
    def _():
        width = coefficient.shape[1] * 2 // BLOCKS
        for p in range(BLOCKS // 2):
            columns = pl.ds(pl.multiple_of((at[1] ^ p) * width, width), width)
            high[:, columns], low[:, columns] = halves(coefficient[:, p * width : (p + 1) * width])

    a_high, a_low = halves(back[...])
    out[...] = solved[...] - (
        part(a_high, high[...]) + (part(a_high, low[...]) + part(a_low, high[...]))
    )


def finish(at, back, coefficient, solved, total):
    rows, rank = back.shape
    width, unit = solved.shape[1], rows // ROW_STEPS
    return call(
        finish_body,
        ROW_STEPS,
        at,
        [
            (back, (unit, rank), lambda p, at: (p, 0)),
            coefficient,
            (solved, (unit, width), lambda p, at: (p, 0)),
        ]
        + ([] if total is None else [(total, None, None)]),
        [(pltpu.HBM((rows, 2 * width), jnp.float32), (unit, width), lambda p, at: (p, at[0]))],
        [pltpu.VMEM((rank, width), jnp.bfloat16)] * 2,
        6 * rows * rank * width,
        {} if total is None else {4: 0},
    )[0]


def node_body(count, units, at, *refs):
    pieces = refs[:count]
    down_high, down_low, high, low, back_high, back_low, factors = refs[count:]
    rank = down_high.shape[0]
    unit = factors.shape[0] // units
    done = 0
    for piece in pieces:
        for k in range(piece.shape[0] // unit):
            start = pl.multiple_of(at[done + 1], unit)
            factors[pl.ds(start, unit), :] = piece[k * unit : (k + 1) * unit, :]
            done += 1
    for i, child in enumerate((at[0], 1 - at[0])):
        columns = slice(i * rank, (i + 1) * rank)
        block = factors[:, pl.ds(pl.multiple_of(child * rank, rank), rank)]
        high[:, columns], low[:, columns] = halves(block)
    lead_high, lead_low = halves(factors[:, 2 * rank : 3 * rank].T)
    back_high[...], back_low[...] = halves(factors[:, 3 * rank :])
    down = part(lead_high, high[...]) + (
        part(lead_high, low[...]) + part(lead_low, high[...])
    )
    down_high[...], down_low[...] = halves(down)


def node_blocks(pieces, starts, second, rank):
    at = jnp.stack([second] + starts).astype(jnp.int32)
    results = call(
        functools.partial(node_body, len(pieces), len(starts)),
        1,
        at,
        pieces,
        both(rank, 2 * rank)
        + both(2 * rank, 2 * rank, space=pltpu.HBM)
        + both(2 * rank, rank, space=pltpu.HBM),
        [pltpu.VMEM((2 * rank, 4 * rank), jnp.float32)],
        6 * rank * 4 * rank * rank,
    )
    return results[:2], results[2:4], results[4:]


def pair_body(base, high, low, own, *rest):
    pieces, results = rest[:-2], rest[-2:]
    held, width = pieces[0].shape[1], min(pieces[0].shape[1], results[0].shape[1])
    at = 0
    for result in results[::-1]:
        for start in range(0, result.shape[1], width):
            piece = pieces[at // held][:, at % held : at % held + width]
            result[:, start : start + width] = pair_product(
                high[...], low[...], own[:, at : at + width], piece
            )
            at += width


def reduce_pair(base, down, own, pieces):
    rank, size = own.shape
    return call(
        pair_body,
        1,
        base,
        [*down, own, *pieces],
        [f32(rank, size // 2)] * 2,
        [],
        12 * rank * rank * size,
    )


def couple_body(base, high, low, own, *rest):
    pieces, out = rest[:-1], rest[-1]
    width = pieces[0].shape[1]
    for i, piece in enumerate(pieces):
        columns = slice(i * width, (i + 1) * width)
        out[:, columns] = pair_product(high[...], low[...], own[:, columns], piece[...])


def couple(base, inverse, own, pieces):
    rank, size = own.shape
    return call(
        couple_body, 1, base, [*inverse, own, *pieces], [pltpu.HBM((2 * rank, size), jnp.float32)], [], 24 * rank * rank * size
    )[0]


def quarter_body(base, high, low, own, other, *quarters):
    reduced = pair_product(high[...], low[...], own[...], other[...])
    rows, width = quarters[0].shape
    for i, quarter in enumerate(quarters):
        row, column = divmod(i, 2)
        quarter[...] = reduced[row * rows : (row + 1) * rows, column * width : (column + 1) * width]


def reduce_quarters(base, down, own, other):
    rank, size = own.shape
    return call(
        quarter_body,
        1,
        base,
        [*down, own, other],
        [f32(rank // 2, size // 2)] * len(RINGS),
        [],
        12 * rank * rank * size,
    )


def back_body(base, high, low, coupled, *rest):
    coefficients, out = rest[:-1], rest[-1]
    at = 0
    for coefficient in coefficients:
        columns = slice(at, at + coefficient.shape[1])
        out[:, columns] = coupled[:, columns] - product(high[...], low[...], coefficient[...])
        at += coefficient.shape[1]


def back_substitute(base, back, coupled, coefficients, child):
    rank = back[0].shape[1]
    size = coupled.shape[1]
    rows = lambda p, base: (child, 0)
    return call(
        back_body,
        1,
        base,
        [(back[0], (rank, rank), rows), (back[1], (rank, rank), rows), (coupled, (rank, size), rows), *coefficients],
        [f32(rank, size)],
        [],
        6 * rank * rank * size,
    )[0]


def split_body(node, value, high, low):
    high[...], low[...] = halves(value[...])


def top_body(places, node, high, low, *rest):
    pieces, (out, c_high, c_low) = rest[:-3], rest[-3:]
    rows, width = pieces[0].shape
    for piece, (row, column, nodes) in zip(pieces, places):
        for at, mask in enumerate(nodes):
            start = pl.multiple_of((node[0] ^ mask) * 2 * rows + row * rows, rows)
            block = halves(piece[at * rows : (at + 1) * rows, :])
            columns = slice(column * width, (column + 1) * width)
            c_high[pl.ds(start, rows), columns], c_low[pl.ds(start, rows), columns] = block
    out[...] = part(high[...], c_high[...]) + (
        part(high[...], c_low[...]) + part(low[...], c_high[...])
    )


def solve_top(node, inverse, pieces, places):
    rank, order = inverse[0].shape
    width = 2 * pieces[0].shape[1]
    return call(
        functools.partial(top_body, places),
        1,
        node,
        [*inverse, *pieces],
        [f32(rank, width)],
        [pltpu.VMEM((order, width), jnp.bfloat16)] * 2,
        6 * rank * order * width,
    )[0]


def shards(
    shots, leaf_inverse, leaf_basis, leaf_back, level_one, level_two, level_three, top_inverse
):
    rank = leaf_basis.shape[0]
    place = lax.axis_index("leaf")
    core, near, far = place & 1, place >> 1 & 1, place >> 2 & 1
    base = jnp.reshape(core << 2 | (near ^ far) << 1 | far, (1,)).astype(jnp.int32)
    node = jnp.reshape(place // TREE, (1,)).astype(jnp.int32)

    half = jnp.stack([core, base[0] & 3]).astype(jnp.int32)
    other_half = jnp.stack([1 - core, base[0] & 3]).astype(jnp.int32)

    groups = [list(range(i, i + TREE)) for i in range(0, lax.axis_size("leaf"), TREE)]
    gather = functools.partial(
        lax.all_gather, axis_name="leaf", axis_index_groups=groups, axis=0, tiled=True
    )
    one_other = swap(level_one, CORE)
    two_near = swap(level_two, X_NEAR)
    three_near, three_far = swap(level_three, X_NEAR), swap(level_three, X_FAR)

    high, low, *sent = reduce_lead(base, leaf_basis, leaf_inverse, shots)
    other = [swap(piece, CORE) for piece in sent]
    own = reduce_own(base, high, low, shots)
    down_1, inverse_1, back_1 = node_blocks(
        [level_one, one_other], [0 * core, 0 * core + rank], core, rank
    )
    own, two_near, three_near, three_far = lax.optimization_barrier(
        (own, two_near, three_near, three_far)
    )
    sent, own_1 = reduce_pair(base, down_1, own, other)
    other_1 = swap(sent, X_NEAR)
    solved = [solve_leaf(half, leaf_inverse, after(shots, sent), pltpu.HBM)]
    three_near = after(three_near, sent)
    three_both = swap(three_near, X_FAR)
    other_1, three_both, solved[0] = lax.optimization_barrier((other_1, three_both, solved[0]))

    rows_2, rows_3 = level_two.shape[0], level_three.shape[0]
    two = [level_two, swap(level_two, CORE), two_near, swap(two_near, CORE)]
    starts = [core * rows_2, (1 - core) * rows_2]
    down_2, inverse_2, back_2 = node_blocks(
        two, starts + [rank + start for start in starts], near, rank
    )
    sent, own_2 = reduce_pair(base, down_2, own_1, [other_1])
    other_2 = swap(sent, X_FAR)
    top = gather(after(top_inverse, sent))
    own, other, own_1, other_1 = after((own, other, own_1, other_1), sent)
    coupled_1 = couple(base, inverse_1, own, other)
    coupled_2 = couple(base, inverse_2, own_1, [other_1])
    three = [level_three, three_near, three_far, three_both]
    three += [swap(value, CORE) for value in three]
    starts = []
    for flip in (0, X_FAR, CORE, X_FAR | CORE):
        for mask in (0, X_NEAR):
            seat = place ^ mask ^ flip
            starts.append(((seat ^ far << 2) >> 2 & 1) * rank + (seat & 3) * rows_3)
    down_3, inverse_3, back_3 = node_blocks(three, starts, far, rank)
    quarters = reduce_quarters(base, down_3, own_2, other_2)

    held, order = [[quarter] for quarter in quarters], [[0] for _ in RINGS]
    for step in range(len(RINGS)):
        sent = [jnp.concatenate(parts, 0) if step else parts[0] for parts in held]
        if step == len(RINGS) - 1:
            sent[-1], top = lax.optimization_barrier((sent[-1], top))
        for quarter in range(len(RINGS)):
            way = RINGS[(quarter + step) % len(RINGS)]
            held[quarter].append(swap(sent[quarter], way))
            order[quarter] += [mask ^ way for mask in order[quarter]]
        if step == 0:
            coupled_3 = couple(base, inverse_3, own_2, [other_2])
    unit = rank // ROW_STEPS
    block = ((unit, top.shape[1]), lambda p, node: (p, 0))
    top_rows = call(
        split_body,
        ROW_STEPS,
        node,
        [(hbm(top), *block)],
        [(value, *block) for value in both(*top.shape)],
        [],
        rank * top.shape[1],
    )
    pieces, places = [], []
    for quarter, parts in enumerate(held):
        row, column = divmod(quarter, 2)
        at = 0
        for value in parts:
            count = value.shape[0] // (rank // 2)
            pieces.append(value)
            places.append((row, column, [mask // TREE for mask in order[quarter][at : at + count]]))
            at += count
    coefficients = [solve_top(node, top_rows, pieces, places)]
    levels = ((coupled_3, back_3, X_FAR), (coupled_2, back_2, X_NEAR), (coupled_1, back_1, CORE))
    for coupled, back, mask in levels:
        sent = back_substitute(base, back, coupled, coefficients, 1)
        other = swap(sent, mask)
        own = back_substitute(base, back, coupled, coefficients, 0)
        if mask == X_NEAR:
            solved.append(solve_leaf(other_half, leaf_inverse, after(shots, sent), jax.ShapeDtypeStruct))
            other, solved[1] = lax.optimization_barrier((other, solved[1]))
        coefficients = [own, other]
    total = finish(half, leaf_back, own, solved[0], None)
    return finish(other_half, leaf_back, other, solved[1], total)


def solution(mesh):
    return jax.shard_map(
        shards,
        mesh=mesh,
        in_specs=(P("leaf", None),) * 8,
        out_specs=P("leaf", None),
        check_vma=False,
    )
```

time: 536 us -> 152 us (0.28)
  waiting for transfers between devices: 373 us -> 15.8 us
  matrix products: 102 us -> 0 us
  Pallas kernels: 0 us -> 70.9 us
  between operations: 0.6 us -> 14 us
  other arithmetic: 12.4 us -> 3.71 us
  local copies, waits for them, and re-layouts: 0.07 us -> 5.87 us
    ppermute x22 -> x36, waiting for transfers between devices: 373 us -> 15.7 us  [swap(): lax.ppermute(value, 'leaf', [(i, i ^ mask) for i in range(lax.axis_size('...]
    dot_general x16 -> x0, matrix products: 102 us -> none  [the longest x1 29.9 us: shards(): solved = jnp.dot(leaf_inverse, shots, precision=highest)]
    pallas_call x0 -> x23, Pallas kernels: none -> 70.9 us  [call(): pl.pallas_call(body, grid_spec=pltpu.PrefetchScalarGridSpec(num_scalar_pr...]
    select_n x8 -> x0, other arithmetic: 10 us -> none  [the longest x3 5.06 us: collect_nodes(): jnp.where(upper_half, jnp.concatenate([partner, values], 0), jnp.concaten...]
    unnamed x30 -> x74, local copies, waits for them, and re-layouts: 0.07 us -> 5.7 us
    ppermute x22 -> x36, starting transfers between devices: 43.2 us -> 41.3 us  [swap(): lax.ppermute(value, 'leaf', [(i, i ^ mask) for i in range(lax.axis_size('...]
  transfers between devices with their start and end apart: 22 -> 37, of which waited for: 21 -> 8; matrix products, arithmetic and copies ran while one was open for 2% -> 3% of each run, Pallas kernels for 0% -> 40%
where the time goes in v2:
time: 152 us; the launch traced here: 151 us
  Pallas kernels  70.9 us (47%)
  starting transfers between devices  41.3 us (27%)
  waiting for transfers between devices  15.8 us (10%)
  between operations  14 us (9%)
  local copies, waits for them, and re-layouts  5.87 us (4%)
  other arithmetic  3.71 us (2%)
    pallas_call x23, Pallas kernels, call(): pl.pallas_call(body, grid_spec=pltpu.PrefetchScalarGridSpec(num_scalar_pr...  70.9 us
    ppermute x36, starting transfers between devices, swap(): lax.ppermute(value, 'leaf', [(i, i ^ mask) for i in range(lax.axis_size('...  41.3 us
    ppermute x36, waiting for transfers between devices, swap(): lax.ppermute(value, 'leaf', [(i, i ^ mask) for i in range(lax.axis_size('...  15.7 us
    unnamed x74, local copies, waits for them, and re-layouts  5.7 us
    concatenate x12, other arithmetic, shards(): sent = [jnp.concatenate(parts, 0) if step else parts[0] for parts in held]  3.48 us
  transfers between devices with their start and end apart: 37, of which 8 were waited for; matrix products, arithmetic and copies ran while one was open for 3% of the time, Pallas kernels for 40%

profile of v2, /device:TPU:1, one launch (start us, length us, event | category | flops | bytes accessed | tf_op | source)
XLA Modules:
  0.0 151.5 jit_solution(16184807374103154013)
XLA Ops:
  9.4 2.6 %collective-permute-start.3 = (f32[64,1024]{1,0:T(8,128)}, f32[64,1024]{1,0:T(8,128)S(1)}, u32[]{:S(2)}, u32[]{:S(2)}) collective-permute-start(f32[64,1024]{1,0:T(8,128)} %refs_0_.5), channel_id=1, source_target_pairs={{0,6},{1,7},{2,4},{3,5},{4,2},{5,3},{6,0},{7,1},{8,14},{9,15},{10,... | collective-permute-start | bytes 786440 | tf_op jit(solution)/shard_map/ppermute | solution.py:18
  13.2 8.2 %shard_map.83 = (bf16[256,1024]{1,0:T(8,128)(2,1)S(1)}, bf16[256,1024]{1,0:T(8,128)(2,1)S(1)}, f32[256,256]{1,0:T(8,128)}, f32[256,256]{1,0:T(8,128)S(1)}, f32[2...) custom-call(s32[1]{0:T(128)} %bitcast.2.base, f32[256,1024]{1,0:T(8,128)S(1)} %copy-done.12, f32[1024,1024]{1,0:T(8,128)} %inverse.5, ...), custom_call_target="tpu_custom_call" | custom-call | flops 3221225472 | bytes 16777216 | tf_op jit(solution)/shard_map/pallas_call | solution.py:57
  23.9 3.4 %collective-permute-done.2.refs_1_ = f32[64,1024]{1,0:T(8,128)S(1)} collective-permute-done((f32[64,1024]{1,0:T(8,128)}, f32[64,1024]{1,0:T(8,128)S(1)}, u32[]{:S(2)}, u32[]{:S(2)}) %collective-permute-start.2) | collective-permute-done | bytes 262176 | tf_op jit(solution)/shard_map/ppermute | solution.py:18
  28.7 4.5 %shard_map.84.own = f32[256,1024]{1,0:T(8,128)S(1)} custom-call(s32[1]{0:T(128)} %bitcast.2.base, bf16[256,1024]{1,0:T(8,128)(2,1)S(1)} %get-tuple-element.65.high, bf16[256,1024]{1,0:T(8,128)(2,1)S(1)} %get-tuple-element.66.low, f32[1024,2048]{1,0:T(8,128)} %shots.5), custom_call_target="tpu_custom_call" | custom-call | flops 1610612736 | bytes 11534336 | tf_op jit(solution)/shard_map/pallas_call | solution.py:57
  33.4 2.2 %shard_map.82 = (bf16[256,512]{1,0:T(8,128)(2,1)S(1)}, bf16[256,512]{1,0:T(8,128)(2,1)S(1)}, bf16[512,512]{1,0:T(8,128)(2,1)}, bf16[512,512]{1,0:T(8,128)(2,1)},...) custom-call(s32[3]{0:T(128)S(1)} %pad_add_fusion.1.at, f32[256,1024]{1,0:T(8,128)S(1)} %copy-done.7, ...), custom_call_target="tpu_custom_call" | custom-call | flops 402653184 | bytes 6291456 | tf_op jit(solution)/shard_map/pallas_call | solution.py:57
  38.5 1.9 %collective-permute-start.9 = (f32[64,1024]{1,0:T(8,128)S(1)}, f32[64,1024]{1,0:T(8,128)S(1)}, u32[]{:S(2)}, u32[]{:S(2)}) collective-permute-start(f32[64,1024]{1,0:T(8,128)S(1)} %collective-permute-done.2.refs_1_), channel_id=1, source_target_pairs={{0,6},{1,7},{2,4},{3,5},{4,2},{5,3},{6,0},{7,1},{8,14},{9,15},{10,... | collective-permute-start | bytes 786440 | tf_op jit(solution)/shard_map/ppermute | solution.py:18
  40.4 12.0 %shard_map.86.solved = f32[1024,1024]{1,0:T(8,128)} custom-call(s32[2]{0:T(128)S(1)} %pad_add_fusion.2.half.at, f32[1024,1024]{1,0:T(8,128)} %inverse.5, f32[1024,2048]{1,0:T(8,128)} %shots.5), custom_call_target="tpu_custom_call" | custom-call | flops 6442450944 | bytes 16777216 | tf_op jit(solution)/shard_map/pallas_call | solution.py:57
  52.4 2.3 %shard_map.87 = (bf16[256,512]{1,0:T(8,128)(2,1)S(1)}, bf16[256,512]{1,0:T(8,128)(2,1)S(1)}, bf16[512,512]{1,0:T(8,128)(2,1)}, bf16[512,512]{1,0:T(8,128)(2,1)},...) custom-call(s32[5]{0:T(128)S(1)} %stack.79.at, f32[128,1024]{1,0:T(8,128)S(1)} %copy-done.17, ...), custom_call_target="tpu_custom_call" | custom-call | flops 402653184 | bytes 6291456 | tf_op jit(solution)/shard_map/pallas_call | solution.py:57
  58.6 3.2 %shard_map.91 = (bf16[256,512]{1,0:T(8,128)(2,1)S(1)}, bf16[256,512]{1,0:T(8,128)(2,1)S(1)}, bf16[512,512]{1,0:T(8,128)(2,1)}, bf16[512,512]{1,0:T(8,128)(2,1)},...) custom-call(s32[9]{0:T(128)S(1)} %stack.89.at, f32[64,1024]{1,0:T(8,128)S(1)} %copy-done.22, ...), custom_call_target="tpu_custom_call" | custom-call | flops 402653184 | bytes 6291456 | tf_op jit(solution)/shard_map/pallas_call | solution.py:57
  61.8 4.7 %collective-permute-done.16.rest_0_.other = f32[256,256]{1,0:T(8,128)S(1)} collective-permute-done((f32[256,256]{1,0:T(8,128)}, f32[256,256]{1,0:T(8,128)S(1)}, u32[]{:S(2)}, u32[]{:S(2)}) %collective-permute-start.16) | collective-permute-done | bytes 262176 | tf_op jit(solution)/shard_map/ppermute | solution.py:18
  66.9 3.8 %collective-permute-start.17 = (f32[128,128]{1,0:T(8,128)S(1)}, f32[128,128]{1,0:T(8,128)S(1)}, u32[]{:S(2)}, u32[]{:S(2)}) collective-permute-start(f32[128,128]{1,0:T(8,128)S(1)} %get-tuple-element.104.rest_15_), channel_id=1, source_target_pairs={{0,96},{1,97},{2,98},{3,99},{4,100},{5,101},{6,102},{7,103},{8,104... | collective-permute-start | bytes 196616 | tf_op jit(solution)/shard_map/ppermute | solution.py:18
  72.0 1.9 %collective-permute-start.28 = (f32[128,128]{1,0:T(8,128)S(1)}, f32[128,128]{1,0:T(8,128)S(1)}, u32[]{:S(2)}, u32[]{:S(2)}) collective-permute-start(f32[128,128]{1,0:T(8,128)S(1)} %get-tuple-element.111.rest_10_), channel_id=1, source_target_pairs={{0,24},{1,25},{2,26},{3,27},{4,28},{5,29},{6,30},{7,31},{8,16},{9,... | collective-permute-start | bytes 196616 | tf_op jit(solution)/shard_map/ppermute | solution.py:18
  79.1 2.3 %collective-permute-start.22 = (f32[512,128]{1,0:T(8,128)S(1)}, f32[512,128]{1,0:T(8,128)S(1)}, u32[]{:S(2)}, u32[]{:S(2)}) collective-permute-start(f32[512,128]{1,0:T(8,128)S(1)} %pad_maximum_fusion.5), channel_id=1, source_target_pairs={{0,24},{1,25},{2,26},{3,27},{4,28},{5,29},{6,30},{7,31},{8,16},{9,... | collective-permute-start | bytes 786440 | tf_op jit(solution)/shard_map/ppermute | solution.py:18
  83.9 4.4 %collective-permute-done.22.rest_3_ = f32[512,128]{1,0:T(8,128)S(1)} collective-permute-done((f32[512,128]{1,0:T(8,128)S(1)}, f32[512,128]{1,0:T(8,128)S(1)}, u32[]{:S(2)}, u32[]{:S(2)}) %collective-permute-start.22) | collective-permute-done | bytes 262176 | tf_op jit(solution)/shard_map/ppermute | solution.py:18
  93.7 2.1 %collective-permute-start.32 = (f32[1024,128]{1,0:T(8,128)}, f32[1024,128]{1,0:T(8,128)}, u32[]{:S(2)}, u32[]{:S(2)}) collective-permute-start(f32[1024,128]{1,0:T(8,128)} %pad_maximum_fusion), channel_id=1, source_target_pairs={{0,24},{1,25},{2,26},{3,27},{4,28},{5,29},{6,30},{7,31},{8,16},{9,... | collective-permute-start | bytes 1572872 | tf_op jit(solution)/shard_map/ppermute | solution.py:18
  99.4 3.2 %shard_map.94 = (bf16[256,4096]{1,0:T(8,128)(2,1)S(1)}, bf16[256,4096]{1,0:T(8,128)(2,1)S(1)}) custom-call(s32[1]{0:T(128)} %bitcast.18.node, f32[256,4096]{1,0:T(8,128)} %all-gather.2.cloned.1.call-done.value), custom_call_target="tpu_custom_call" | custom-call | flops 1048576 | bytes 12582912 | tf_op jit(solution)/shard_map/pallas_call | solution.py:57
  102.6 2.4 %collective-permute-done.32.rest_19_ = f32[1024,128]{1,0:T(8,128)} collective-permute-done((f32[1024,128]{1,0:T(8,128)}, f32[1024,128]{1,0:T(8,128)}, u32[]{:S(2)}, u32[]{:S(2)}) %collective-permute-start.32) | collective-permute-done | bytes 524320 | tf_op jit(solution)/shard_map/ppermute | solution.py:18
  105.0 4.3 %shard_map.95.rest_0_ = f32[256,256]{1,0:T(8,128)S(1)} custom-call(s32[1]{0:T(128)} %bitcast.18.node, bf16[256,4096]{1,0:T(8,128)(2,1)S(1)} %get-tuple-element.107.high, bf16[256,4096]{1,0:T(8,128)(2,1)S(1)} %get-tuple-element.108.low, f32[128,128]{1,0:T(8,128)S(1)} %get-tuple-element.109.rest_0_, f32[128,128]{1,0:T(8,128)S(1)} %collective-permute-done.20.rest_1_, ...), custom_call_target="tpu_custom_call" | custom-call | flops 1610612736 | bytes 12845056 | tf_op jit(solution)/shard_map/pallas_call | solution.py:57
  110.9 2.0 %shard_map.90.coupled = f32[512,512]{1,0:T(8,128)} custom-call(s32[1]{0:T(128)} %bitcast.2.base, bf16[512,512]{1,0:T(8,128)(2,1)S(1)} %copy-done.20, bf16[512,512]{1,0:T(8,128)(2,1)S(1)} %copy-done.21, f32[256,512]{1,0:T(8,128)S(1)} %get-tuple-element.93.own, f32[256,512]{1,0:T(8,128)S(1)} %collective-permute-done.8.rest_0_), custom_call_target="tpu_custom_call" | custom-call | flops 805306368 | bytes 4194304 | tf_op jit(solution)/shard_map/pallas_call | solution.py:57
  112.9 3.1 %shard_map.89.coupled = f32[512,1024]{1,0:T(8,128)} custom-call(s32[1]{0:T(128)} %bitcast.2.base, bf16[512,512]{1,0:T(8,128)(2,1)S(1)} %copy-done.23, bf16[512,512]{1,0:T(8,128)(2,1)S(1)} %copy-done.24, f32[256,1024]{1,0:T(8,128)S(1)} %copy-done.14, f32[256,256]{1,0:T(8,128)S(1)} %copy-done.26, f32[256,256]{1,0:T(8,128)S(1)} %copy-done.28, ...), custom_call_target="tpu_custom_call" | custom-call | flops 1610612736 | bytes 6291456 | tf_op jit(solution)/shard_map/pallas_call | solution.py:57
  117.4 11.2 %shard_map.100.solved = f32[1024,1024]{1,0:T(8,128)S(1)} custom-call(s32[2]{0:T(128)S(1)} %pad_add_fusion.half.at, f32[1024,1024]{1,0:T(8,128)} %inverse.5, f32[1024,2048]{1,0:T(8,128)} %shots.5), custom_call_target="tpu_custom_call" | custom-call | flops 6442450944 | bytes 16777216 | tf_op jit(solution)/shard_map/pallas_call | solution.py:57
  129.2 5.8 %collective-permute-start.35 = (f32[256,1024]{1,0:T(8,128)S(1)}, f32[256,1024]{1,0:T(8,128)S(1)}, u32[]{:S(2)}, u32[]{:S(2)}) collective-permute-start(f32[256,1024]{1,0:T(8,128)S(1)} %shard_map.101), channel_id=1, source_target_pairs={{0,1},{1,0},{2,3},{3,2},{4,5},{5,4},{6,7},{7,6},{8,9},{9,8},{10,11... | collective-permute-start | bytes 3145736 | tf_op jit(solution)/shard_map/ppermute | solution.py:18
  135.7 4.5 %shard_map.103.rest_0_ = f32[1024,2048]{1,0:T(8,128)} custom-call(s32[2]{0:T(128)S(1)} %pad_add_fusion.2.half.at, f32[1024,256]{1,0:T(8,128)S(1)} %copy-done.4, f32[256,1024]{1,0:T(8,128)S(1)} %shard_map.102.coefficient, f32[1024,1024]{1,0:T(8,128)S(1)} %copy-done.3), custom_call_target="tpu_custom_call" | custom-call | flops 1610612736 | bytes 14680064 | tf_op jit(solution)/shard_map/pallas_call | solution.py:57
  140.2 4.5 %shard_map.104 = f32[1024,2048]{1,0:T(8,128)} custom-call(s32[2]{0:T(128)S(1)} %pad_add_fusion.half.at, f32[1024,256]{1,0:T(8,128)S(1)} %copy-done.4, f32[256,1024]{1,0:T(8,128)S(1)} %collective-permute-done.35.coefficient, f32[1024,1024]{1,0:T(8,128)S(1)} %shard_map.100.solved, f32[1024,2048]{1,0:T(8,128)} %shard_map.103.rest_0_), custom_call_target="tpu_custom_call", output_to_operand_aliasing={{}: (4, {})} | custom-call | flops 1610612736 | bytes 23068672 | tf_op jit(solution)/shard_map/pallas_call | solution.py:57
  (165 shorter events, 37.3 us)
Async XLA Ops:
  6.5 87.2 %all-gather.2.cloned.1.call-start = ((), (), s32[]{:S(2)}) async-start(), calls=%async_computation | async-start | bytes 4718592 | tf_op jit(solution)/shard_map/all_gather | solution.py:392
  6.5 26.7 %collective-permute-start = (f32[256,1024]{1,0:T(8,128)}, f32[256,1024]{1,0:T(8,128)S(1)}, u32[]{:S(2)}, u32[]{:S(2)}) collective-permute-start(f32[256,1024]{1,0:T(8,128)} %refs_0_.3), channel_id=1, source_target_pairs={{0,1},{1,0},{2,3},{3,2},{4,5},{5,4},{6,7},{7,6},{8,9},{9,8},{10,11... | collective-permute-start | bytes 3145736 | tf_op jit(solution)/shard_map/ppermute | solution.py:18
  8.0 20.2 %collective-permute-start.1 = (f32[128,1024]{1,0:T(8,128)}, f32[128,1024]{1,0:T(8,128)S(1)}, u32[]{:S(2)}, u32[]{:S(2)}) collective-permute-start(f32[128,1024]{1,0:T(8,128)} %refs_0_.4), channel_id=1, source_target_pairs={{0,2},{1,3},{2,0},{3,1},{4,6},{5,7},{6,4},{7,5},{8,10},{9,11},{10,... | collective-permute-start | bytes 1572872 | tf_op jit(solution)/shard_map/ppermute | solution.py:18
  9.3 18.1 %collective-permute-start.2 = (f32[64,1024]{1,0:T(8,128)}, f32[64,1024]{1,0:T(8,128)S(1)}, u32[]{:S(2)}, u32[]{:S(2)}) collective-permute-start(f32[64,1024]{1,0:T(8,128)} %refs_0_.5), channel_id=1, source_target_pairs={{0,2},{1,3},{2,0},{3,1},{4,6},{5,7},{6,4},{7,5},{8,10},{9,11},{10,... | collective-permute-start | bytes 786440 | tf_op jit(solution)/shard_map/ppermute | solution.py:18
  9.4 18.7 %collective-permute-start.3 = (f32[64,1024]{1,0:T(8,128)}, f32[64,1024]{1,0:T(8,128)S(1)}, u32[]{:S(2)}, u32[]{:S(2)}) collective-permute-start(f32[64,1024]{1,0:T(8,128)} %refs_0_.5), channel_id=1, source_target_pairs={{0,6},{1,7},{2,4},{3,5},{4,2},{5,3},{6,0},{7,1},{8,14},{9,15},{10,... | collective-permute-start | bytes 786440 | tf_op jit(solution)/shard_map/ppermute | solution.py:18
  22.9 12.7 %collective-permute-start.4 = (f32[256,256]{1,0:T(8,128)}, f32[256,256]{1,0:T(8,128)S(1)}, u32[]{:S(2)}, u32[]{:S(2)}) collective-permute-start(f32[256,256]{1,0:T(8,128)} %get-tuple-element.68), channel_id=1, source_target_pairs={{0,1},{1,0},{2,3},{3,2},{4,5},{5,4},{6,7},{7,6},{8,9},{9,8},{10,11... | collective-permute-start | bytes 786440 | tf_op jit(solution)/shard_map/ppermute | solution.py:18
  27.3 8.7 %collective-permute-start.5 = (f32[256,256]{1,0:T(8,128)}, f32[256,256]{1,0:T(8,128)S(1)}, u32[]{:S(2)}, u32[]{:S(2)}) collective-permute-start(f32[256,256]{1,0:T(8,128)} %copy-done.36), channel_id=1, source_target_pairs={{0,1},{1,0},{2,3},{3,2},{4,5},{5,4},{6,7},{7,6},{8,9},{9,8},{10,11... | collective-permute-start | bytes 786440 | tf_op jit(solution)/shard_map/ppermute | solution.py:18
  28.1 7.9 %collective-permute-start.6 = (f32[256,256]{1,0:T(8,128)}, f32[256,256]{1,0:T(8,128)S(1)}, u32[]{:S(2)}, u32[]{:S(2)}) collective-permute-start(f32[256,256]{1,0:T(8,128)} %copy-done.35), channel_id=1, source_target_pairs={{0,1},{1,0},{2,3},{3,2},{4,5},{5,4},{6,7},{7,6},{8,9},{9,8},{10,11... | collective-permute-start | bytes 786440 | tf_op jit(solution)/shard_map/ppermute | solution.py:18
  28.1 8.0 %collective-permute-start.7 = (f32[256,256]{1,0:T(8,128)}, f32[256,256]{1,0:T(8,128)S(1)}, u32[]{:S(2)}, u32[]{:S(2)}) collective-permute-start(f32[256,256]{1,0:T(8,128)} %copy-done.34), channel_id=1, source_target_pairs={{0,1},{1,0},{2,3},{3,2},{4,5},{5,4},{6,7},{7,6},{8,9},{9,8},{10,11... | collective-permute-start | bytes 786440 | tf_op jit(solution)/shard_map/ppermute | solution.py:18
  33.2 19.2 %collective-permute-start.10 = (f32[128,1024]{1,0:T(8,128)S(1)}, f32[128,1024]{1,0:T(8,128)S(1)}, u32[]{:S(2)}, u32[]{:S(2)}) collective-permute-start(f32[128,1024]{1,0:T(8,128)S(1)} %copy-done.17), channel_id=1, source_target_pairs={{0,1},{1,0},{2,3},{3,2},{4,5},{5,4},{6,7},{7,6},{8,9},{9,8},{10,11... | collective-permute-start | bytes 1572872 | tf_op jit(solution)/shard_map/ppermute | solution.py:18
  35.6 16.8 %collective-permute-start.11 = (f32[128,1024]{1,0:T(8,128)S(1)}, f32[128,1024]{1,0:T(8,128)S(1)}, u32[]{:S(2)}, u32[]{:S(2)}) collective-permute-start(f32[128,1024]{1,0:T(8,128)S(1)} %collective-permute-done.1.refs_2_), channel_id=1, source_target_pairs={{0,1},{1,0},{2,3},{3,2},{4,5},{5,4},{6,7},{7,6},{8,9},{9,8},{10,11... | collective-permute-start | bytes 1572872 | tf_op jit(solution)/shard_map/ppermute | solution.py:18
  37.2 17.5 %collective-permute-start.8 = (f32[256,512]{1,0:T(8,128)S(1)}, f32[256,512]{1,0:T(8,128)S(1)}, u32[]{:S(2)}, u32[]{:S(2)}) collective-permute-start(f32[256,512]{1,0:T(8,128)S(1)} %get-tuple-element.75), channel_id=1, source_target_pairs={{0,2},{1,3},{2,0},{3,1},{4,6},{5,7},{6,4},{7,5},{8,10},{9,11},{10,... | collective-permute-start | bytes 1572872 | tf_op jit(solution)/shard_map/ppermute | solution.py:18
  38.5 16.1 %collective-permute-start.9 = (f32[64,1024]{1,0:T(8,128)S(1)}, f32[64,1024]{1,0:T(8,128)S(1)}, u32[]{:S(2)}, u32[]{:S(2)}) collective-permute-start(f32[64,1024]{1,0:T(8,128)S(1)} %collective-permute-done.2.refs_1_), channel_id=1, source_target_pairs={{0,6},{1,7},{2,4},{3,5},{4,2},{5,3},{6,0},{7,1},{8,14},{9,15},{10,... | collective-permute-start | bytes 786440 | tf_op jit(solution)/shard_map/ppermute | solution.py:18
  57.1 9.4 %collective-permute-start.16 = (f32[256,256]{1,0:T(8,128)}, f32[256,256]{1,0:T(8,128)S(1)}, u32[]{:S(2)}, u32[]{:S(2)}) collective-permute-start(f32[256,256]{1,0:T(8,128)} %copy-done.33), channel_id=1, source_target_pairs={{0,6},{1,7},{2,4},{3,5},{4,2},{5,3},{6,0},{7,1},{8,14},{9,15},{10,... | collective-permute-start | bytes 786440 | tf_op jit(solution)/shard_map/ppermute | solution.py:18
  73.9 9.8 %collective-permute-start.18 = (f32[256,128]{1,0:T(8,128)S(1)}, f32[256,128]{1,0:T(8,128)S(1)}, u32[]{:S(2)}, u32[]{:S(2)}) collective-permute-start(f32[256,128]{1,0:T(8,128)S(1)} %pad_maximum_fusion.8), channel_id=1, source_target_pairs={{0,8},{1,9},{2,10},{3,11},{4,12},{5,13},{6,14},{7,15},{8,0},{9,1},... | collective-permute-start | bytes 393224 | tf_op jit(solution)/shard_map/ppermute | solution.py:18
  79.1 9.2 %collective-permute-start.22 = (f32[512,128]{1,0:T(8,128)S(1)}, f32[512,128]{1,0:T(8,128)S(1)}, u32[]{:S(2)}, u32[]{:S(2)}) collective-permute-start(f32[512,128]{1,0:T(8,128)S(1)} %pad_maximum_fusion.5), channel_id=1, source_target_pairs={{0,24},{1,25},{2,26},{3,27},{4,28},{5,29},{6,30},{7,31},{8,16},{9,... | collective-permute-start | bytes 786440 | tf_op jit(solution)/shard_map/ppermute | solution.py:18
  81.5 7.6 %collective-permute-start.26 = (f32[512,128]{1,0:T(8,128)S(1)}, f32[512,128]{1,0:T(8,128)S(1)}, u32[]{:S(2)}, u32[]{:S(2)}) collective-permute-start(f32[512,128]{1,0:T(8,128)S(1)} %pad_maximum_fusion.6), channel_id=1, source_target_pairs={{0,96},{1,97},{2,98},{3,99},{4,100},{5,101},{6,102},{7,103},{8,104... | collective-permute-start | bytes 786440 | tf_op jit(solution)/shard_map/ppermute | solution.py:18
  83.8 8.4 %collective-permute-start.19 = (f32[512,128]{1,0:T(8,128)S(1)}, f32[512,128]{1,0:T(8,128)S(1)}, u32[]{:S(2)}, u32[]{:S(2)}) collective-permute-start(f32[512,128]{1,0:T(8,128)S(1)} %pad_maximum_fusion.4), channel_id=1, source_target_pairs={{0,32},{1,33},{2,34},{3,35},{4,36},{5,37},{6,38},{7,39},{8,40},{9,... | collective-permute-start | bytes 786440 | tf_op jit(solution)/shard_map/ppermute | solution.py:18
  89.1 13.5 %collective-permute-start.23 = (f32[1024,128]{1,0:T(8,128)}, f32[1024,128]{1,0:T(8,128)}, u32[]{:S(2)}, u32[]{:S(2)}) collective-permute-start(f32[1024,128]{1,0:T(8,128)} %pad_maximum_fusion.1), channel_id=1, source_target_pairs={{0,96},{1,97},{2,98},{3,99},{4,100},{5,101},{6,102},{7,103},{8,104... | collective-permute-start | bytes 1572872 | tf_op jit(solution)/shard_map/ppermute | solution.py:18
  89.9 12.6 %collective-permute-start.27 = (f32[1024,128]{1,0:T(8,128)}, f32[1024,128]{1,0:T(8,128)}, u32[]{:S(2)}, u32[]{:S(2)}) collective-permute-start(f32[1024,128]{1,0:T(8,128)} %pad_maximum_fusion.2), channel_id=1, source_target_pairs={{0,8},{1,9},{2,10},{3,11},{4,12},{5,13},{6,14},{7,15},{8,0},{9,1},... | collective-permute-start | bytes 1572872 | tf_op jit(solution)/shard_map/ppermute | solution.py:18
  90.8 11.8 %collective-permute-start.31 = (f32[1024,128]{1,0:T(8,128)}, f32[1024,128]{1,0:T(8,128)}, u32[]{:S(2)}, u32[]{:S(2)}) collective-permute-start(f32[1024,128]{1,0:T(8,128)} %pad_maximum_fusion.3), channel_id=1, source_target_pairs={{0,32},{1,33},{2,34},{3,35},{4,36},{5,37},{6,38},{7,39},{8,40},{9,... | collective-permute-start | bytes 1572872 | tf_op jit(solution)/shard_map/ppermute | solution.py:18
  93.7 11.2 %collective-permute-start.32 = (f32[1024,128]{1,0:T(8,128)}, f32[1024,128]{1,0:T(8,128)}, u32[]{:S(2)}, u32[]{:S(2)}) collective-permute-start(f32[1024,128]{1,0:T(8,128)} %pad_maximum_fusion), channel_id=1, source_target_pairs={{0,24},{1,25},{2,26},{3,27},{4,28},{5,29},{6,30},{7,31},{8,16},{9,... | collective-permute-start | bytes 1572872 | tf_op jit(solution)/shard_map/ppermute | solution.py:18
  116.8 11.7 %collective-permute-start.34 = (f32[256,512]{1,0:T(8,128)S(1)}, f32[256,512]{1,0:T(8,128)S(1)}, u32[]{:S(2)}, u32[]{:S(2)}) collective-permute-start(f32[256,512]{1,0:T(8,128)S(1)} %shard_map.99), channel_id=1, source_target_pairs={{0,2},{1,3},{2,0},{3,1},{4,6},{5,7},{6,4},{7,5},{8,10},{9,11},{10,... | collective-permute-start | bytes 1572872 | tf_op jit(solution)/shard_map/ppermute | solution.py:18
  129.2 10.9 %collective-permute-start.35 = (f32[256,1024]{1,0:T(8,128)S(1)}, f32[256,1024]{1,0:T(8,128)S(1)}, u32[]{:S(2)}, u32[]{:S(2)}) collective-permute-start(f32[256,1024]{1,0:T(8,128)S(1)} %shard_map.101), channel_id=1, source_target_pairs={{0,1},{1,0},{2,3},{3,2},{4,5},{5,4},{6,7},{7,6},{8,9},{9,8},{10,11... | collective-permute-start | bytes 3145736 | tf_op jit(solution)/shard_map/ppermute | solution.py:18
  (50 other events, 222.8 us)
Sparse Core Ops, SparseCore 0:
  55.4 32.9 all-gather.1

commit v3 on v2

--- a/solution.py
+++ b/solution.py
@@ -82,7 +82,8 @@
     return [space(shape, jnp.bfloat16)] * 2
 
 
-def lead_body(base, basis, inverse, shots, high, low, *pieces):
+def reduce_body(base, basis, inverse, shots, *refs):
+    pieces, (own, high, low) = refs[:-3], refs[-3:]
     p = pl.program_id(0)
 
     @pl.when(p == 0)
@@ -96,37 +97,30 @@
         def _():
             piece[...] = reduced
 
-
-def reduce_lead(base, basis, inverse, shots):
+    @pl.when(p >= len(pieces))
+    def _():
+        own[...] = reduced
+
+
+def reduce_leaf(base, basis, inverse, shots):
     rank, rows = basis.shape
     width, half = shots.shape[1] // BLOCKS, BLOCKS // 2
     return call(
-        lead_body,
-        half,
+        reduce_body,
+        BLOCKS,
         base,
-        [basis, hbm(inverse), (hbm(shots), (rows, width), lambda p, base: (0, base[0] ^ (p + half)))],
-        both(rank, rows) + [f32(rank, width)] * half,
-        [],
-        6 * rank * rows * (rows + half * width),
-    )
-
-
-def reduce_body(base, high, low, shots, out):
-    out[...] = product(high[...], low[...], shots[...])
-
-
-def reduce_own(base, high, low, shots):
-    rank, rows = high.shape
-    width, half = shots.shape[1] // BLOCKS, BLOCKS // 2
-    return call(
-        reduce_body,
-        half,
-        base,
-        [high, low, (hbm(shots), (rows, width), lambda p, base: (0, base[0] ^ p))],
-        [(f32(rank, half * width), (rank, width), lambda p, base: (0, p))],
-        [],
-        6 * rank * rows * half * width,
-    )[0]
+        [hbm(basis), hbm(inverse), (hbm(shots), (rows, width), lambda p, base: (0, base[0] ^ (p + half) % BLOCKS))],
+        [f32(rank, width)] * half
+        + [
+            (
+                pltpu.HBM((rank, half * width), jnp.float32),
+                (rank, width),
+                lambda p, base: (0, jnp.maximum(p - half, 0)),
+            )
+        ],
+        [pltpu.VMEM((rank, rows), jnp.bfloat16)] * 2,
+        6 * rank * rows * (rows + shots.shape[1]),
+    )
 
 
 def leaf_body(half, inverse, shots, out, high, low):
@@ -365,16 +359,15 @@
     two_near = swap(level_two, X_NEAR)
     three_near, three_far = swap(level_three, X_NEAR), swap(level_three, X_FAR)
 
-    high, low, *sent = reduce_lead(base, leaf_basis, leaf_inverse, shots)
+    *sent, own = reduce_leaf(base, leaf_basis, leaf_inverse, shots)
     other = [swap(piece, CORE) for piece in sent]
-    own = reduce_own(base, high, low, shots)
     down_1, inverse_1, back_1 = node_blocks(
         [level_one, one_other], [0 * core, 0 * core + rank], core, rank
     )
     own, two_near, three_near, three_far = lax.optimization_barrier(
         (own, two_near, three_near, three_far)
     )
-    sent, own_1 = reduce_pair(base, down_1, own, other)
+    sent, own_1 = reduce_pair(base, down_1, hbm(own), other)
     other_1 = swap(sent, X_NEAR)
     solved = [solve_leaf(half, leaf_inverse, after(shots, sent), pltpu.HBM)]
     three_near = after(three_near, sent)
@@ -391,7 +384,7 @@
     other_2 = swap(sent, X_FAR)
     top = gather(after(top_inverse, sent))
     own, other, own_1, other_1 = after((own, other, own_1, other_1), sent)
-    coupled_1 = couple(base, inverse_1, own, other)
+    coupled_1 = couple(base, inverse_1, hbm(own), other)
     coupled_2 = couple(base, inverse_2, own_1, [other_1])
     three = [level_three, three_near, three_far, three_both]
     three += [swap(value, CORE) for value in three]

time: 152 us -> 149 us (0.980)
  waiting for transfers between devices: 15.8 us -> 11.1 us
  Pallas kernels: 70.9 us -> 73.9 us
    ppermute x36, waiting for transfers between devices: 15.7 us -> 11 us  [swap(): lax.ppermute(value, 'leaf', [(i, i ^ mask) for i in range(lax.axis_size('...]
    pallas_call x23 -> x22, Pallas kernels: 70.9 us -> 73.9 us  [call(): pl.pallas_call(body, grid_spec=pltpu.PrefetchScalarGridSpec(num_scalar_pr...]
    unnamed x74 -> x64, local copies, waits for them, and re-layouts: 5.7 us -> 5.78 us
  transfers between devices with their start and end apart: 37 -> 37, of which waited for: 8 -> 9; matrix products, arithmetic and copies ran while one was open for 3% -> 3% of each run, Pallas kernels for 40% -> 43%
where the time goes in v3:
time: 149 us
  Pallas kernels  73.9 us (50%)
  starting transfers between devices  40.3 us (27%)
  between operations  13.9 us (9%)
  waiting for transfers between devices  11.1 us (7%)
  local copies, waits for them, and re-layouts  5.95 us (4%)
  other arithmetic  3.69 us (2%)
    pallas_call x22, Pallas kernels, call(): pl.pallas_call(body, grid_spec=pltpu.PrefetchScalarGridSpec(num_scalar_pr...  73.9 us
    ppermute x36, starting transfers between devices, swap(): lax.ppermute(value, 'leaf', [(i, i ^ mask) for i in range(lax.axis_size('...  40.3 us
    ppermute x36, waiting for transfers between devices, swap(): lax.ppermute(value, 'leaf', [(i, i ^ mask) for i in range(lax.axis_size('...  11 us
    unnamed x64, local copies, waits for them, and re-layouts  5.78 us
    concatenate x12, other arithmetic, shards(): sent = [jnp.concatenate(parts, 0) if step else parts[0] for parts in held]  3.46 us
  transfers between devices with their start and end apart: 37, of which 9 were waited for; matrix products, arithmetic and copies ran while one was open for 3% of the time, Pallas kernels for 43%

profile of v3, /device:TPU:1, one launch (start us, length us, event | category | flops | bytes accessed | tf_op | source)
XLA Modules:
  0.0 148.7 jit_solution(8828388478939280567)
XLA Ops:
  9.4 2.6 %collective-permute-start.3 = (f32[64,1024]{1,0:T(8,128)}, f32[64,1024]{1,0:T(8,128)}, u32[]{:S(2)}, u32[]{:S(2)}) collective-permute-start(f32[64,1024]{1,0:T(8,128)} %refs_0_.5), channel_id=1, source_target_pairs={{0,6},{1,7},{2,4},{3,5},{4,2},{5,3},{6,0},{7,1},{8,14},{9,15},{10,... | collective-permute-start | bytes 786440 | tf_op jit(solution)/shard_map/ppermute | solution.py:18
  12.0 12.8 %shard_map.83 = (f32[256,256]{1,0:T(8,128)}, f32[256,256]{1,0:T(8,128)S(1)}, f32[256,256]{1,0:T(8,128)S(1)}, f32[256,256]{1,0:T(8,128)S(1)}, f32[256,1024]{1,0:T(8,128)}) custom-call(s32[1]{0:T(128)} %bitcast.2.base, f32[256,1024]{1,0:T(8,128)} %basis.1, f32[1024,1024]{1,0:T(8,128)} %inverse.5, f32[1024,2048]{1,0:T(8,128)} %shots.3), custom_call_target="tpu_custom_call" | custom-call | flops 4831838208 | bytes 15728640 | tf_op jit(solution)/shard_map/pallas_call | solution.py:57
  29.1 2.2 %shard_map.82 = (bf16[256,512]{1,0:T(8,128)(2,1)S(1)}, bf16[256,512]{1,0:T(8,128)(2,1)S(1)}, bf16[512,512]{1,0:T(8,128)(2,1)}, bf16[512,512]{1,0:T(8,128)(2,1)},...) custom-call(s32[3]{0:T(128)S(1)} %pad_add_fusion.1.at, f32[256,1024]{1,0:T(8,128)S(1)} %copy-done.7, ...), custom_call_target="tpu_custom_call" | custom-call | flops 402653184 | bytes 6291456 | tf_op jit(solution)/shard_map/pallas_call | solution.py:57
  31.6 2.5 %shard_map.84 = (f32[256,512]{1,0:T(8,128)S(1)}, f32[256,512]{1,0:T(8,128)S(1)}) custom-call(s32[1]{0:T(128)} %bitcast.2.base, bf16[256,512]{1,0:T(8,128)(2,1)S(1)} %get-tuple-element.70.high, bf16[256,512]{1,0:T(8,128)(2,1)S(1)} %get-tuple-element.71.low, f32[256,1024]{1,0:T(8,128)} %get-tuple-element.82.own, f32[256,256]{1,0:T(8,128)} %collective-permute-done.4.rest_0_, ...), custom_call_target="tpu_custom_call" | custom-call | flops 805306368 | bytes 4194304 | tf_op jit(solution)/shard_map/pallas_call | solution.py:57
  35.6 1.9 %collective-permute-start.9 = (f32[64,1024]{1,0:T(8,128)S(1)}, f32[64,1024]{1,0:T(8,128)S(1)}, u32[]{:S(2)}, u32[]{:S(2)}) collective-permute-start(f32[64,1024]{1,0:T(8,128)S(1)} %collective-permute-done.2.refs_1_), channel_id=1, source_target_pairs={{0,6},{1,7},{2,4},{3,5},{4,2},{5,3},{6,0},{7,1},{8,14},{9,15},{10,... | collective-permute-start | bytes 786440 | tf_op jit(solution)/shard_map/ppermute | solution.py:18
  37.5 12.0 %shard_map.85.solved = f32[1024,1024]{1,0:T(8,128)} custom-call(s32[2]{0:T(128)S(1)} %pad_add_fusion.2.half.at, f32[1024,1024]{1,0:T(8,128)} %inverse.5, f32[1024,2048]{1,0:T(8,128)} %shots.3), custom_call_target="tpu_custom_call" | custom-call | flops 6442450944 | bytes 16777216 | tf_op jit(solution)/shard_map/pallas_call | solution.py:57
  49.4 2.2 %shard_map.86 = (bf16[256,512]{1,0:T(8,128)(2,1)S(1)}, bf16[256,512]{1,0:T(8,128)(2,1)S(1)}, bf16[512,512]{1,0:T(8,128)(2,1)}, bf16[512,512]{1,0:T(8,128)(2,1)},...) custom-call(s32[5]{0:T(128)S(1)} %stack.79.at, f32[128,1024]{1,0:T(8,128)S(1)} %copy-done.14, ...), custom_call_target="tpu_custom_call" | custom-call | flops 402653184 | bytes 6291456 | tf_op jit(solution)/shard_map/pallas_call | solution.py:57
  56.0 3.2 %shard_map.90 = (bf16[256,512]{1,0:T(8,128)(2,1)S(1)}, bf16[256,512]{1,0:T(8,128)(2,1)S(1)}, bf16[512,512]{1,0:T(8,128)(2,1)}, bf16[512,512]{1,0:T(8,128)(2,1)},...) custom-call(s32[9]{0:T(128)S(1)} %stack.89.at, f32[64,1024]{1,0:T(8,128)S(1)} %copy-done.19, ...), custom_call_target="tpu_custom_call" | custom-call | flops 402653184 | bytes 6291456 | tf_op jit(solution)/shard_map/pallas_call | solution.py:57
  59.2 4.0 %collective-permute-done.16.rest_0_.other = f32[256,256]{1,0:T(8,128)S(1)} collective-permute-done((f32[256,256]{1,0:T(8,128)}, f32[256,256]{1,0:T(8,128)S(1)}, u32[]{:S(2)}, u32[]{:S(2)}) %collective-permute-start.16) | collective-permute-done | bytes 262176 | tf_op jit(solution)/shard_map/ppermute | solution.py:18
  63.6 3.8 %collective-permute-start.17 = (f32[128,128]{1,0:T(8,128)S(1)}, f32[128,128]{1,0:T(8,128)S(1)}, u32[]{:S(2)}, u32[]{:S(2)}) collective-permute-start(f32[128,128]{1,0:T(8,128)S(1)} %get-tuple-element.102.rest_15_), channel_id=1, source_target_pairs={{0,96},{1,97},{2,98},{3,99},{4,100},{5,101},{6,102},{7,103},{8,104... | collective-permute-start | bytes 196616 | tf_op jit(solution)/shard_map/ppermute | solution.py:18
  68.8 1.9 %collective-permute-start.28 = (f32[128,128]{1,0:T(8,128)S(1)}, f32[128,128]{1,0:T(8,128)S(1)}, u32[]{:S(2)}, u32[]{:S(2)}) collective-permute-start(f32[128,128]{1,0:T(8,128)S(1)} %get-tuple-element.109.rest_10_), channel_id=1, source_target_pairs={{0,24},{1,25},{2,26},{3,27},{4,28},{5,29},{6,30},{7,31},{8,16},{9,... | collective-permute-start | bytes 196616 | tf_op jit(solution)/shard_map/ppermute | solution.py:18
  71.2 1.5 %collective-permute-start.21 = (f32[256,128]{1,0:T(8,128)S(1)}, f32[256,128]{1,0:T(8,128)S(1)}, u32[]{:S(2)}, u32[]{:S(2)}) collective-permute-start(f32[256,128]{1,0:T(8,128)S(1)} %pad_maximum_fusion.9), channel_id=1, source_target_pairs={{0,32},{1,33},{2,34},{3,35},{4,36},{5,37},{6,38},{7,39},{8,40},{9,... | collective-permute-start | bytes 393224 | tf_op jit(solution)/shard_map/ppermute | solution.py:18
  76.0 2.2 %collective-permute-start.22 = (f32[512,128]{1,0:T(8,128)S(1)}, f32[512,128]{1,0:T(8,128)S(1)}, u32[]{:S(2)}, u32[]{:S(2)}) collective-permute-start(f32[512,128]{1,0:T(8,128)S(1)} %pad_maximum_fusion.5), channel_id=1, source_target_pairs={{0,24},{1,25},{2,26},{3,27},{4,28},{5,29},{6,30},{7,31},{8,16},{9,... | collective-permute-start | bytes 786440 | tf_op jit(solution)/shard_map/ppermute | solution.py:18
  78.3 1.7 %collective-permute-start.26 = (f32[512,128]{1,0:T(8,128)S(1)}, f32[512,128]{1,0:T(8,128)S(1)}, u32[]{:S(2)}, u32[]{:S(2)}) collective-permute-start(f32[512,128]{1,0:T(8,128)S(1)} %pad_maximum_fusion.6), channel_id=1, source_target_pairs={{0,96},{1,97},{2,98},{3,99},{4,100},{5,101},{6,102},{7,103},{8,104... | collective-permute-start | bytes 786440 | tf_op jit(solution)/shard_map/ppermute | solution.py:18
  80.6 4.5 %collective-permute-done.22.rest_3_ = f32[512,128]{1,0:T(8,128)S(1)} collective-permute-done((f32[512,128]{1,0:T(8,128)S(1)}, f32[512,128]{1,0:T(8,128)S(1)}, u32[]{:S(2)}, u32[]{:S(2)}) %collective-permute-start.22) | collective-permute-done | bytes 262176 | tf_op jit(solution)/shard_map/ppermute | solution.py:18
  90.5 2.1 %collective-permute-start.32 = (f32[1024,128]{1,0:T(8,128)}, f32[1024,128]{1,0:T(8,128)}, u32[]{:S(2)}, u32[]{:S(2)}) collective-permute-start(f32[1024,128]{1,0:T(8,128)} %pad_maximum_fusion), channel_id=1, source_target_pairs={{0,24},{1,25},{2,26},{3,27},{4,28},{5,29},{6,30},{7,31},{8,16},{9,... | collective-permute-start | bytes 1572872 | tf_op jit(solution)/shard_map/ppermute | solution.py:18
  96.1 3.2 %shard_map.93 = (bf16[256,4096]{1,0:T(8,128)(2,1)S(1)}, bf16[256,4096]{1,0:T(8,128)(2,1)S(1)}) custom-call(s32[1]{0:T(128)} %bitcast.18.node, f32[256,4096]{1,0:T(8,128)} %all-gather.2.cloned.1.call-done.value), custom_call_target="tpu_custom_call" | custom-call | flops 1048576 | bytes 12582912 | tf_op jit(solution)/shard_map/pallas_call | solution.py:57
  100.7 4.3 %shard_map.94.rest_0_ = f32[256,256]{1,0:T(8,128)S(1)} custom-call(s32[1]{0:T(128)} %bitcast.18.node, bf16[256,4096]{1,0:T(8,128)(2,1)S(1)} %get-tuple-element.105.high, bf16[256,4096]{1,0:T(8,128)(2,1)S(1)} %get-tuple-element.106.low, f32[128,128]{1,0:T(8,128)S(1)} %get-tuple-element.107.rest_0_, f32[128,128]{1,0:T(8,128)S(1)} %collective-permute-done.20.rest_1_, ...), custom_call_target="tpu_custom_call" | custom-call | flops 1610612736 | bytes 12845056 | tf_op jit(solution)/shard_map/pallas_call | solution.py:57
  106.3 2.0 %shard_map.89.coupled = f32[512,512]{1,0:T(8,128)} custom-call(s32[1]{0:T(128)} %bitcast.2.base, bf16[512,512]{1,0:T(8,128)(2,1)S(1)} %copy-done.17, bf16[512,512]{1,0:T(8,128)(2,1)S(1)} %copy-done.18, f32[256,512]{1,0:T(8,128)S(1)} %get-tuple-element.91.own, f32[256,512]{1,0:T(8,128)S(1)} %collective-permute-done.8.rest_0_), custom_call_target="tpu_custom_call" | custom-call | flops 805306368 | bytes 4194304 | tf_op jit(solution)/shard_map/pallas_call | solution.py:57
  108.3 4.5 %shard_map.88.coupled = f32[512,1024]{1,0:T(8,128)} custom-call(s32[1]{0:T(128)} %bitcast.2.base, bf16[512,512]{1,0:T(8,128)(2,1)S(1)} %copy-done.20, bf16[512,512]{1,0:T(8,128)(2,1)S(1)} %copy-done.21, f32[256,1024]{1,0:T(8,128)} %get-tuple-element.82.own, f32[256,256]{1,0:T(8,128)} %collective-permute-done.4.rest_0_, f32[256,256]{1,0:T(8,128)S(1)} %copy-done.23, ...), custom_call_target="tpu_custom_call" | custom-call | flops 1610612736 | bytes 6291456 | tf_op jit(solution)/shard_map/pallas_call | solution.py:57
  114.3 11.2 %shard_map.99.solved = f32[1024,1024]{1,0:T(8,128)S(1)} custom-call(s32[2]{0:T(128)S(1)} %pad_add_fusion.half.at, f32[1024,1024]{1,0:T(8,128)} %inverse.5, f32[1024,2048]{1,0:T(8,128)} %shots.3), custom_call_target="tpu_custom_call" | custom-call | flops 6442450944 | bytes 16777216 | tf_op jit(solution)/shard_map/pallas_call | solution.py:57
  126.2 6.1 %collective-permute-start.35 = (f32[256,1024]{1,0:T(8,128)S(1)}, f32[256,1024]{1,0:T(8,128)S(1)}, u32[]{:S(2)}, u32[]{:S(2)}) collective-permute-start(f32[256,1024]{1,0:T(8,128)S(1)} %shard_map.100), channel_id=1, source_target_pairs={{0,1},{1,0},{2,3},{3,2},{4,5},{5,4},{6,7},{7,6},{8,9},{9,8},{10,11... | collective-permute-start | bytes 3145736 | tf_op jit(solution)/shard_map/ppermute | solution.py:18
  132.9 4.5 %shard_map.102.rest_0_ = f32[1024,2048]{1,0:T(8,128)} custom-call(s32[2]{0:T(128)S(1)} %pad_add_fusion.2.half.at, f32[1024,256]{1,0:T(8,128)S(1)} %copy-done.4, f32[256,1024]{1,0:T(8,128)S(1)} %shard_map.101.coefficient, f32[1024,1024]{1,0:T(8,128)S(1)} %copy-done.3), custom_call_target="tpu_custom_call" | custom-call | flops 1610612736 | bytes 14680064 | tf_op jit(solution)/shard_map/pallas_call | solution.py:57
  137.4 4.5 %shard_map.103 = f32[1024,2048]{1,0:T(8,128)} custom-call(s32[2]{0:T(128)S(1)} %pad_add_fusion.half.at, f32[1024,256]{1,0:T(8,128)S(1)} %copy-done.4, f32[256,1024]{1,0:T(8,128)S(1)} %collective-permute-done.35.coefficient, f32[1024,1024]{1,0:T(8,128)S(1)} %shard_map.99.solved, f32[1024,2048]{1,0:T(8,128)} %shard_map.102.rest_0_), custom_call_target="tpu_custom_call", output_to_operand_aliasing={{}: (4, {})} | custom-call | flops 1610612736 | bytes 23068672 | tf_op jit(solution)/shard_map/pallas_call | solution.py:57
  (154 shorter events, 33.5 us)
Async XLA Ops:
  6.5 84.0 %all-gather.2.cloned.1.call-start = ((), (), s32[]{:S(2)}) async-start(), calls=%async_computation | async-start | bytes 4718592 | tf_op jit(solution)/shard_map/all_gather | solution.py:385
  6.5 22.3 %collective-permute-start = (f32[256,1024]{1,0:T(8,128)}, f32[256,1024]{1,0:T(8,128)S(1)}, u32[]{:S(2)}, u32[]{:S(2)}) collective-permute-start(f32[256,1024]{1,0:T(8,128)} %refs_0_.3), channel_id=1, source_target_pairs={{0,1},{1,0},{2,3},{3,2},{4,5},{5,4},{6,7},{7,6},{8,9},{9,8},{10,11... | collective-permute-start | bytes 3145736 | tf_op jit(solution)/shard_map/ppermute | solution.py:18
  8.0 20.4 %collective-permute-start.1 = (f32[128,1024]{1,0:T(8,128)}, f32[128,1024]{1,0:T(8,128)S(1)}, u32[]{:S(2)}, u32[]{:S(2)}) collective-permute-start(f32[128,1024]{1,0:T(8,128)} %refs_0_.4), channel_id=1, source_target_pairs={{0,2},{1,3},{2,0},{3,1},{4,6},{5,7},{6,4},{7,5},{8,10},{9,11},{10,... | collective-permute-start | bytes 1572872 | tf_op jit(solution)/shard_map/ppermute | solution.py:18
  9.3 18.6 %collective-permute-start.2 = (f32[64,1024]{1,0:T(8,128)}, f32[64,1024]{1,0:T(8,128)S(1)}, u32[]{:S(2)}, u32[]{:S(2)}) collective-permute-start(f32[64,1024]{1,0:T(8,128)} %refs_0_.5), channel_id=1, source_target_pairs={{0,2},{1,3},{2,0},{3,1},{4,6},{5,7},{6,4},{7,5},{8,10},{9,11},{10,... | collective-permute-start | bytes 786440 | tf_op jit(solution)/shard_map/ppermute | solution.py:18
  9.4 18.7 %collective-permute-start.3 = (f32[64,1024]{1,0:T(8,128)}, f32[64,1024]{1,0:T(8,128)}, u32[]{:S(2)}, u32[]{:S(2)}) collective-permute-start(f32[64,1024]{1,0:T(8,128)} %refs_0_.5), channel_id=1, source_target_pairs={{0,6},{1,7},{2,4},{3,5},{4,2},{5,3},{6,0},{7,1},{8,14},{9,15},{10,... | collective-permute-start | bytes 786440 | tf_op jit(solution)/shard_map/ppermute | solution.py:18
  28.8 20.6 %collective-permute-start.10 = (f32[128,1024]{1,0:T(8,128)S(1)}, f32[128,1024]{1,0:T(8,128)S(1)}, u32[]{:S(2)}, u32[]{:S(2)}) collective-permute-start(f32[128,1024]{1,0:T(8,128)S(1)} %copy-done.14), channel_id=1, source_target_pairs={{0,1},{1,0},{2,3},{3,2},{4,5},{5,4},{6,7},{7,6},{8,9},{9,8},{10,11... | collective-permute-start | bytes 1572872 | tf_op jit(solution)/shard_map/ppermute | solution.py:18
  31.3 18.1 %collective-permute-start.11 = (f32[128,1024]{1,0:T(8,128)S(1)}, f32[128,1024]{1,0:T(8,128)S(1)}, u32[]{:S(2)}, u32[]{:S(2)}) collective-permute-start(f32[128,1024]{1,0:T(8,128)S(1)} %collective-permute-done.1.refs_2_), channel_id=1, source_target_pairs={{0,1},{1,0},{2,3},{3,2},{4,5},{5,4},{6,7},{7,6},{8,9},{9,8},{10,11... | collective-permute-start | bytes 1572872 | tf_op jit(solution)/shard_map/ppermute | solution.py:18
  34.2 17.5 %collective-permute-start.8 = (f32[256,512]{1,0:T(8,128)S(1)}, f32[256,512]{1,0:T(8,128)S(1)}, u32[]{:S(2)}, u32[]{:S(2)}) collective-permute-start(f32[256,512]{1,0:T(8,128)S(1)} %get-tuple-element.73), channel_id=1, source_target_pairs={{0,2},{1,3},{2,0},{3,1},{4,6},{5,7},{6,4},{7,5},{8,10},{9,11},{10,... | collective-permute-start | bytes 1572872 | tf_op jit(solution)/shard_map/ppermute | solution.py:18
  35.6 16.1 %collective-permute-start.9 = (f32[64,1024]{1,0:T(8,128)S(1)}, f32[64,1024]{1,0:T(8,128)S(1)}, u32[]{:S(2)}, u32[]{:S(2)}) collective-permute-start(f32[64,1024]{1,0:T(8,128)S(1)} %collective-permute-done.2.refs_1_), channel_id=1, source_target_pairs={{0,6},{1,7},{2,4},{3,5},{4,2},{5,3},{6,0},{7,1},{8,14},{9,15},{10,... | collective-permute-start | bytes 786440 | tf_op jit(solution)/shard_map/ppermute | solution.py:18
  54.4 8.9 %collective-permute-start.16 = (f32[256,256]{1,0:T(8,128)}, f32[256,256]{1,0:T(8,128)S(1)}, u32[]{:S(2)}, u32[]{:S(2)}) collective-permute-start(f32[256,256]{1,0:T(8,128)} %copy-done.28), channel_id=1, source_target_pairs={{0,6},{1,7},{2,4},{3,5},{4,2},{5,3},{6,0},{7,1},{8,14},{9,15},{10,... | collective-permute-start | bytes 786440 | tf_op jit(solution)/shard_map/ppermute | solution.py:18
  63.6 7.0 %collective-permute-start.17 = (f32[128,128]{1,0:T(8,128)S(1)}, f32[128,128]{1,0:T(8,128)S(1)}, u32[]{:S(2)}, u32[]{:S(2)}) collective-permute-start(f32[128,128]{1,0:T(8,128)S(1)} %get-tuple-element.102.rest_15_), channel_id=1, source_target_pairs={{0,96},{1,97},{2,98},{3,99},{4,100},{5,101},{6,102},{7,103},{8,104... | collective-permute-start | bytes 196616 | tf_op jit(solution)/shard_map/ppermute | solution.py:18
  70.7 9.8 %collective-permute-start.18 = (f32[256,128]{1,0:T(8,128)S(1)}, f32[256,128]{1,0:T(8,128)S(1)}, u32[]{:S(2)}, u32[]{:S(2)}) collective-permute-start(f32[256,128]{1,0:T(8,128)S(1)} %pad_maximum_fusion.8), channel_id=1, source_target_pairs={{0,8},{1,9},{2,10},{3,11},{4,12},{5,13},{6,14},{7,15},{8,0},{9,1},... | collective-permute-start | bytes 393224 | tf_op jit(solution)/shard_map/ppermute | solution.py:18
  74.3 5.7 %collective-permute-start.29 = (f32[256,128]{1,0:T(8,128)S(1)}, f32[256,128]{1,0:T(8,128)S(1)}, u32[]{:S(2)}, u32[]{:S(2)}) collective-permute-start(f32[256,128]{1,0:T(8,128)S(1)} %pad_maximum_fusion.11), channel_id=1, source_target_pairs={{0,96},{1,97},{2,98},{3,99},{4,100},{5,101},{6,102},{7,103},{8,104... | collective-permute-start | bytes 393224 | tf_op jit(solution)/shard_map/ppermute | solution.py:18
  76.0 9.2 %collective-permute-start.22 = (f32[512,128]{1,0:T(8,128)S(1)}, f32[512,128]{1,0:T(8,128)S(1)}, u32[]{:S(2)}, u32[]{:S(2)}) collective-permute-start(f32[512,128]{1,0:T(8,128)S(1)} %pad_maximum_fusion.5), channel_id=1, source_target_pairs={{0,24},{1,25},{2,26},{3,27},{4,28},{5,29},{6,30},{7,31},{8,16},{9,... | collective-permute-start | bytes 786440 | tf_op jit(solution)/shard_map/ppermute | solution.py:18
  78.3 7.7 %collective-permute-start.26 = (f32[512,128]{1,0:T(8,128)S(1)}, f32[512,128]{1,0:T(8,128)S(1)}, u32[]{:S(2)}, u32[]{:S(2)}) collective-permute-start(f32[512,128]{1,0:T(8,128)S(1)} %pad_maximum_fusion.6), channel_id=1, source_target_pairs={{0,96},{1,97},{2,98},{3,99},{4,100},{5,101},{6,102},{7,103},{8,104... | collective-permute-start | bytes 786440 | tf_op jit(solution)/shard_map/ppermute | solution.py:18
  80.0 7.1 %collective-permute-start.30 = (f32[512,128]{1,0:T(8,128)S(1)}, f32[512,128]{1,0:T(8,128)S(1)}, u32[]{:S(2)}, u32[]{:S(2)}) collective-permute-start(f32[512,128]{1,0:T(8,128)S(1)} %pad_maximum_fusion.7), channel_id=1, source_target_pairs={{0,8},{1,9},{2,10},{3,11},{4,12},{5,13},{6,14},{7,15},{8,0},{9,1},... | collective-permute-start | bytes 786440 | tf_op jit(solution)/shard_map/ppermute | solution.py:18
  80.5 8.4 %collective-permute-start.19 = (f32[512,128]{1,0:T(8,128)S(1)}, f32[512,128]{1,0:T(8,128)S(1)}, u32[]{:S(2)}, u32[]{:S(2)}) collective-permute-start(f32[512,128]{1,0:T(8,128)S(1)} %pad_maximum_fusion.4), channel_id=1, source_target_pairs={{0,32},{1,33},{2,34},{3,35},{4,36},{5,37},{6,38},{7,39},{8,40},{9,... | collective-permute-start | bytes 786440 | tf_op jit(solution)/shard_map/ppermute | solution.py:18
  86.0 13.7 %collective-permute-start.23 = (f32[1024,128]{1,0:T(8,128)}, f32[1024,128]{1,0:T(8,128)}, u32[]{:S(2)}, u32[]{:S(2)}) collective-permute-start(f32[1024,128]{1,0:T(8,128)} %pad_maximum_fusion.1), channel_id=1, source_target_pairs={{0,96},{1,97},{2,98},{3,99},{4,100},{5,101},{6,102},{7,103},{8,104... | collective-permute-start | bytes 1572872 | tf_op jit(solution)/shard_map/ppermute | solution.py:18
  86.8 12.9 %collective-permute-start.27 = (f32[1024,128]{1,0:T(8,128)}, f32[1024,128]{1,0:T(8,128)}, u32[]{:S(2)}, u32[]{:S(2)}) collective-permute-start(f32[1024,128]{1,0:T(8,128)} %pad_maximum_fusion.2), channel_id=1, source_target_pairs={{0,8},{1,9},{2,10},{3,11},{4,12},{5,13},{6,14},{7,15},{8,0},{9,1},... | collective-permute-start | bytes 1572872 | tf_op jit(solution)/shard_map/ppermute | solution.py:18
  88.0 11.8 %collective-permute-start.31 = (f32[1024,128]{1,0:T(8,128)}, f32[1024,128]{1,0:T(8,128)}, u32[]{:S(2)}, u32[]{:S(2)}) collective-permute-start(f32[1024,128]{1,0:T(8,128)} %pad_maximum_fusion.3), channel_id=1, source_target_pairs={{0,32},{1,33},{2,34},{3,35},{4,36},{5,37},{6,38},{7,39},{8,40},{9,... | collective-permute-start | bytes 1572872 | tf_op jit(solution)/shard_map/ppermute | solution.py:18
  90.5 10.1 %collective-permute-start.32 = (f32[1024,128]{1,0:T(8,128)}, f32[1024,128]{1,0:T(8,128)}, u32[]{:S(2)}, u32[]{:S(2)}) collective-permute-start(f32[1024,128]{1,0:T(8,128)} %pad_maximum_fusion), channel_id=1, source_target_pairs={{0,24},{1,25},{2,26},{3,27},{4,28},{5,29},{6,30},{7,31},{8,16},{9,... | collective-permute-start | bytes 1572872 | tf_op jit(solution)/shard_map/ppermute | solution.py:18
  105.3 7.8 %collective-permute-start.33 = (f32[256,256]{1,0:T(8,128)S(1)}, f32[256,256]{1,0:T(8,128)S(1)}, u32[]{:S(2)}, u32[]{:S(2)}) collective-permute-start(f32[256,256]{1,0:T(8,128)S(1)} %shard_map.96), channel_id=1, source_target_pairs={{0,6},{1,7},{2,4},{3,5},{4,2},{5,3},{6,0},{7,1},{8,14},{9,15},{10,... | collective-permute-start | bytes 786440 | tf_op jit(solution)/shard_map/ppermute | solution.py:18
  113.6 11.9 %collective-permute-start.34 = (f32[256,512]{1,0:T(8,128)S(1)}, f32[256,512]{1,0:T(8,128)S(1)}, u32[]{:S(2)}, u32[]{:S(2)}) collective-permute-start(f32[256,512]{1,0:T(8,128)S(1)} %shard_map.98), channel_id=1, source_target_pairs={{0,2},{1,3},{2,0},{3,1},{4,6},{5,7},{6,4},{7,5},{8,10},{9,11},{10,... | collective-permute-start | bytes 1572872 | tf_op jit(solution)/shard_map/ppermute | solution.py:18
  126.2 11.2 %collective-permute-start.35 = (f32[256,1024]{1,0:T(8,128)S(1)}, f32[256,1024]{1,0:T(8,128)S(1)}, u32[]{:S(2)}, u32[]{:S(2)}) collective-permute-start(f32[256,1024]{1,0:T(8,128)S(1)} %shard_map.100), channel_id=1, source_target_pairs={{0,1},{1,0},{2,3},{3,2},{4,5},{5,4},{6,7},{7,6},{8,9},{9,8},{10,11... | collective-permute-start | bytes 3145736 | tf_op jit(solution)/shard_map/ppermute | solution.py:18
  (45 other events, 213.1 us)
Sparse Core Ops, SparseCore 0:
  53.2 32.9 all-gather.1
